TPU v7x, 128 devices: a whole 4x4x4 slice. The times are simulated.
128 devices in a mesh: group: 2 (over y_hi), win: 16 (over x, y_lo, core), mp: 4 (over z).
Axes of the slice: x: 4, y: 4 (y_hi: 2, y_lo: 2; y = y_hi * 2 + y_lo), z: 4, core: 2. Of those that a mesh axis runs over, the one named last changes fastest.
Arguments:
- tokens: bfloat16 [2, 4096, 4096], P('group', 'win', 'mp'), may hold values from -7 to 7, as said below
- proj: bfloat16 [2, 4096, 4096], P('group', None, 'mp'), may hold values from -1 to 1, as said below
- cotangent: bfloat16 [4096, 4096], P('win', 'mp'), may hold values from -6 to 6
- counts: int32 [16], P('win'), may hold values from 64 to 256, as said below
- frames: int32 [4096], P('win'), may hold values from 0 to 3, as said below
Outputs:
- input_grads: bfloat16 [2, 4096, 4096], P('group', 'win', 'mp')
- weight_grads: float32 [2, 4096, 4096], P('group', 'win', 'mp')
Inputs may be any that keep to these rules, and one draw needn't show every extreme that they name: Every value lies within the range; proj slot 0 entries scale as 1 / sqrt(1024), slot 1 as 1 / sqrt(4096). `tokens`: finite values. `counts`: some window has all 256 slots live and some window exactly 64. Each window has a token that sees only the first frame and one that sees all frames.
All inputs are finite; a program needn't handle non-finite values.
Results may differ from a plain program's by a relative error of at most 0.015.
The roundings to bfloat16 on the way count: a program that leaves them out, or rounds other values in their place, can miss the bound.
Values may be sent and summed in bfloat16 or wider, within the bound.
A program may use at most 192 MiB of HBM per device.

v0:
```python
import jax
import jax.numpy as jnp
from jax import lax
from jax.sharding import PartitionSpec as P

DV = 1024
HEAD_DIM = 128
FRAMES = 4


def from_behind(shard, axis, by):
    devices = lax.axis_size(axis)
    pairs = [(i, i + by) for i in range(devices) if 0 <= i + by < devices]
    return lax.ppermute(shard, axis, pairs)


def one_head(head_items, allowed):
    queries, key_rows, value_rows, upstream = head_items
    factor = HEAD_DIM ** (-0.5)
    scores = jnp.einsum("qd,kd->qk", queries, key_rows, preferred_element_type=jnp.float32) * factor
    scores = jnp.where(allowed, scores, -1e30)
    top_score = jnp.max(scores, axis=-1, keepdims=True)
    shifted = jnp.exp(scores - top_score)
    attention = shifted / jnp.sum(shifted, axis=-1, keepdims=True)
    rounded = attention.astype(jnp.bfloat16)
    value_grad = jnp.einsum(
        "qk,qd->kd", rounded, upstream, preferred_element_type=jnp.float32
    ).astype(jnp.bfloat16)
    attn_grad = jnp.einsum("qd,kd->qk", upstream, value_rows, preferred_element_type=jnp.float32)
    score_grad = (
        attention * (attn_grad - jnp.sum(attention * attn_grad, axis=-1, keepdims=True)) * factor
    )
    score_grad = score_grad.astype(jnp.bfloat16)
    query_grad = jnp.einsum(
        "qk,kd->qd", score_grad, key_rows, preferred_element_type=jnp.float32
    ).astype(jnp.bfloat16)
    key_grad = jnp.einsum(
        "qk,qd->kd", score_grad, queries, preferred_element_type=jnp.float32
    ).astype(jnp.bfloat16)
    return (query_grad, key_grad, value_grad)


def head_grads(queries, key_rows, value_rows, upstream, allowed):
    head_count = queries.shape[1] // HEAD_DIM

    def split_heads(array):
        return array.reshape(array.shape[0], head_count, HEAD_DIM).transpose(1, 0, 2)

    def merge_heads(array):
        return array.transpose(1, 0, 2).reshape(array.shape[1], head_count * HEAD_DIM)

    def per_head(head_items):
        return one_head(head_items, allowed)

    query_grad, key_grad, value_grad = lax.map(
        per_head,
        (
            split_heads(queries),
            split_heads(key_rows),
            split_heads(value_rows),
            split_heads(upstream),
        ),
    )
    return (merge_heads(query_grad), merge_heads(key_grad), merge_heads(value_grad))


def local(tokens, proj, cotangent, counts, frames):
    group_index = lax.axis_index("group")
    is_video = group_index == 0
    local_rows = tokens[0]
    weight = proj[0]
    row_count = local_rows.shape[0]
    columns = weight.shape[1]
    full_width = weight.shape[0]
    video_rows = row_count * full_width // DV
    gathered = lax.all_gather(local_rows, "mp", axis=1, tiled=True)
    features = gathered.reshape(video_rows, DV)
    w_key = weight[:DV]
    w_value = weight[DV : 2 * DV]

    def video_front():
        key_rows = jnp.dot(features, w_key, preferred_element_type=jnp.float32).astype(jnp.bfloat16)
        value_rows = jnp.dot(features, w_value, preferred_element_type=jnp.float32).astype(
            jnp.bfloat16
        )
        return (
            jnp.concatenate([key_rows, value_rows], 1),
            jnp.zeros((row_count, columns), jnp.bfloat16),
        )

    def neural_front():
        queries = jnp.dot(gathered, weight, preferred_element_type=jnp.float32).astype(jnp.bfloat16)
        return (jnp.zeros((video_rows, 2 * columns), jnp.bfloat16), queries)

    outgoing, queries = lax.cond(is_video, video_front, neural_front)
    arrived = from_behind(outgoing, "group", 1)
    key_rows = arrived[:, :columns]
    value_rows = arrived[:, columns:]
    live_rows = lax.iota(jnp.int32, row_count) < counts[0]
    upstream = jnp.where(live_rows[:, None], cotangent, jnp.zeros_like(cotangent))
    key_frame = lax.iota(jnp.int32, video_rows) // (video_rows // FRAMES)
    allowed = key_frame[None, :] <= frames[:, None]

    def attend():
        return head_grads(queries, key_rows, value_rows, upstream, allowed)

    def neural_input(query_grad):
        return jnp.dot(query_grad, weight.T, preferred_element_type=jnp.float32)

    def neural_weight(query_grad):
        return jnp.dot(gathered.T, query_grad, preferred_element_type=jnp.float32)

    def neural_all():
        query_grad, key_grad, value_grad = attend()
        return (
            jnp.concatenate([key_grad, value_grad], 1),
            query_grad,
            neural_input(query_grad),
            neural_weight(query_grad),
        )

    def video_wait_all():
        return (
            jnp.zeros((video_rows, 2 * columns), jnp.bfloat16),
            jnp.zeros((row_count, columns), jnp.bfloat16),
            jnp.zeros((row_count, full_width), jnp.float32),
            jnp.zeros((full_width, columns), jnp.float32),
        )

    returning, query_grad, early_input, early_weight = lax.cond(
        is_video, video_wait_all, neural_all
    )
    returned = from_behind(returning, "group", -1)

    def video_back():
        key_grad = returned[:, :columns]
        value_grad = returned[:, columns:]
        feature_part = jnp.dot(key_grad, w_key.T, preferred_element_type=jnp.float32)
        feature_part = feature_part + jnp.dot(
            value_grad, w_value.T, preferred_element_type=jnp.float32
        )
        feature_part = feature_part.reshape(row_count, full_width)
        weight_part = jnp.concatenate(
            [
                jnp.dot(features.T, key_grad, preferred_element_type=jnp.float32),
                jnp.dot(features.T, value_grad, preferred_element_type=jnp.float32),
                jnp.zeros((full_width - 2 * DV, columns), jnp.float32),
            ],
            0,
        )
        return (feature_part, weight_part)

    def neural_back():
        return (early_input, early_weight)

    input_part, weight_part = lax.cond(is_video, video_back, neural_back)
    summed = lax.psum_scatter(
        input_part.astype(jnp.bfloat16), "mp", scatter_dimension=1, tiled=True
    ).astype(jnp.float32)
    residual = jnp.where(is_video, jnp.zeros_like(summed), cotangent.astype(jnp.float32))
    input_grads = (summed + residual).astype(jnp.bfloat16)
    weight_grads = lax.psum_scatter(weight_part, "win", scatter_dimension=0, tiled=True)
    return (input_grads[None], weight_grads[None])


def solution(mesh):
    return jax.shard_map(
        local,
        mesh=mesh,
        in_specs=(
            P("group", "win", "mp"),
            P("group", None, "mp"),
            P("win", "mp"),
            P("win"),
            P("win"),
        ),
        out_specs=(P("group", "win", "mp"), P("group", "win", "mp")),
        check_vma=False,
    )
```

profile of v0, /device:TPU:17, one launch (start us, length us, event | category | flops | bytes accessed | tf_op | source)
XLA Modules:
  0.0 588.8 jit_solution(15386314961577830210)
XLA Ops:
  8.0 4.7 slice_bitcast_fusion
  12.7 30.3 %all-gather.3.cloned.1.call-done = bf16[1,256,4096]{2,1,0:T(8,128)(2,1)} async-done(((bf16[1,256,1024]{2,1,0:T(8,128)(2,1)}), bf16[1,256,4096]{2,1,0:T(8,128)(2,1)}) %all-gather.3.cloned.1.call-update) | async-done | bytes 2097168 | tf_op jit(solution)/shard_map/all_gather | solution.py:76
  43.0 4.5 reshape.55
  47.5 7.1 %conditional.3 = (bf16[1024,2048]{0,1:T(8,128)(2,1)S(1)}, bf16[256,1024]{1,0:T(8,128)(2,1)}) conditional(s32[]{:T(128)} %convert_element_type.41, (bf16[256,4096]{1,0:T(8,128)(2,1)S(1)}, bf16[4096,1024]{1,0:T(8,128)(2,1)}) %tuple.116, (bf16[1024,1024]{1,0:T(8,128)(2,1)}, bf16[1024,1024]{1,0:T(8,128)(2,1)}, bf16[1024,1024]{1,0:T(8,128)(2,1)}) %tuple.68), branch_computations={%region_0.0_spmd, %region_1.0_spmd} | conditional | flops 4305453056 | bytes 38273096 | solution.py:95
  47.5 6.6 %convolution_convert_fusion = bf16[256,1024]{1,0:T(8,128)(2,1)} fusion(bf16[256,4096]{1,0:T(8,128)(2,1)S(1)} %get-tuple-element.166, bf16[4096,1024]{1,0:T(8,128)(2,1)} %get-tuple-element.167), kind=kOutput, calls=%fused_computation.1 | convolution fusion | flops 2147745792 | bytes 11010048 | tf_op jit(solution)/shard_map/cond/branch_0_fun/dot_general | solution.py:92
  55.9 93.6 %collective-permute-done = bf16[1024,2048]{0,1:T(8,128)(2,1)} collective-permute-done((bf16[1024,2048]{0,1:T(8,128)(2,1)S(1)}, bf16[1024,2048]{0,1:T(8,128)(2,1)}, u32[]{:S(2)}, u32[]{:S(2)}) %collective-permute-start) | collective-permute-done | bytes 4194336 | tf_op jit(solution)/shard_map/ppermute | solution.py:14
  149.5 92.4 %conditional.4 = (bf16[1024,2048]{1,0:T(8,128)(2,1)S(1)}, bf16[256,4096]{1,0:T(8,128)(2,1)S(1)}, f32[4096,1024]{0,1:T(8,128)}) conditional(s32[]{:T(128)} %convert_element_type.41, (bf16[256,1024]{1,0:T(8,128)(2,1)}, bf16[1024,2048]{0,1:T(8,128)(2,1)}, s32[1]{0:T(128)}, s32[256,1]{0,1:T(1,128)S(1)}, bf16[256,1024]{1,0:T(8,128)(2,1)S(1)}, ...), branch_computations={%region_2.8_spmd, %region_8.9_spmd} | conditional | flops 4644445696 | bytes 113604480 | solution.py:130
  152.8 4.7 fusion.41
  157.5 68.6 %while.24 = (s32[]{:T(128)}, bf16[8,256,128]{1,2,0:T(8,128)(2,1)}, bf16[8,1024,128]{2,1,0:T(8,128)(2,1)}, bf16[8,1024,128]{2,1,0:T(8,128)(2,1)}, bf16[8,256,128]...) while((s32[]{:T(128)}, bf16[8,256,128]{1,2,0:T(8,128)(2,1)}, ...), condition=%wide.region_7.7_spmd.clone, body=%wide.region_3.6_spmd.clone.sunk | while | flops 340819200 | bytes 10834045 | solution.py:55
  159.2 1.4 multiply_reduce_fusion.2
  163.0 2.0 fusion.82
  171.6 2.0 fusion.82
  176.3 1.4 multiply_reduce_fusion.2
  180.2 2.0 fusion.82
  188.7 2.0 fusion.82
  197.3 2.0 fusion.82
  202.1 1.4 multiply_reduce_fusion.2
  205.9 2.0 fusion.82
  210.6 1.4 multiply_reduce_fusion.2
  214.5 2.0 fusion.82
  223.0 2.0 fusion.82
  226.1 3.0 copy_bitcast_fusion
  229.6 1.9 slice-done.1
  231.5 2.4 fusion.42
  233.9 8.1 %convolution_bitcast_fusion = f32[4096,1024]{0,1:T(8,128)} fusion(bf16[256,1024]{0,1:T(8,128)(2,1)S(1)} %bitcast.133, bf16[256,4096]{1,0:T(8,128)(2,1)S(1)} %copy-done.2), kind=kOutput, calls=%fused_computation.51 | convolution fusion | flops 2147483648 | bytes 19398656 | tf_op jit(solution)/shard_map/cond/branch_0_fun/dot_general | solution.py:111
  242.0 1.5 collective-permute-start.1
  243.6 88.3 %collective-permute-done.1 = bf16[1024,2048]{1,0:T(8,128)(2,1)S(1)} collective-permute-done((bf16[1024,2048]{1,0:T(8,128)(2,1)S(1)}, bf16[1024,2048]{1,0:T(8,128)(2,1)S(1)}, u32[]{:S(2)}, u32[]{:S(2)}) %collective-permute-start.1) | collective-permute-done | bytes 4194336 | tf_op jit(solution)/shard_map/ppermute | solution.py:14
  331.8 17.4 %conditional.5 = (bf16[256,4096]{1,0:T(8,128)(2,1)}, f32[4096,1024]{1,0:T(8,128)}) conditional(s32[]{:T(128)} %convert_element_type.41, (bf16[256,4096]{1,0:T(8,128)(2,1)}, f32[4096,1024]{0,1:T(8,128)}) %tuple.118, (bf16[1024,2048]{1,0:T(8,128)(2,1)S(1)}, bf16[1024,1024]{1,0:T(8,128)(2,1)}, bf16[1024,1024]{1,0:T(8,128)(2,1)}, ...), branch_computations={%region_9.10_spmd, %region_10.11_spmd} | conditional | flops 8600420352 | bytes 115392640 | solution.py:156
  331.8 17.4 %copy.22 = f32[4096,1024]{1,0:T(8,128)} copy(f32[4096,1024]{0,1:T(8,128)} %get-tuple-element.263) | data formatting | bytes 33554432 | tf_op jit(solution)/shard_map
  350.0 49.1 %reduce-scatter.3.cloned.1.call-done = bf16[256,1024]{1,0:T(8,128)(2,1)} async-done(((bf16[256,4096]{1,0:T(8,128)(2,1)}), bf16[256,1024]{1,0:T(8,128)(2,1)}) %reduce-scatter.3.cloned.1.call-update) | async-done | bytes 524304 | tf_op jit(solution)/shard_map/reduce_scatter | solution.py:157
  399.1 2.0 fusion.39
  401.2 181.1 %reduce-scatter.5.cloned.1.call-done = f32[256,1024]{1,0:T(8,128)} async-done(((f32[4096,1024]{1,0:T(8,128)}), f32[256,1024]{1,0:T(8,128)}) %reduce-scatter.5.cloned.1.call-update) | async-done | bytes 1048592 | tf_op jit(solution)/shard_map/reduce_scatter | solution.py:162
  (97 shorter events, 53.3 us)
Async XLA Ops:
  7.2 35.8 %all-gather.3.cloned.1.call-start = ((), (), s32[]{:S(2)}) async-start(), calls=%async_computation.4 | async-start | bytes 2621440 | tf_op jit(solution)/shard_map/all_gather | solution.py:76
  7.9 391.2 %reduce-scatter.3.cloned.1.call-start = ((), (), s32[]{:S(2)}) async-start(), calls=%async_computation.2 | async-start | bytes 2621440 | tf_op jit(solution)/shard_map/reduce_scatter | solution.py:157
  43.0 4.5 copy-start
  47.5 102.1 %copy-start.6 = (bf16[256,1024]{1,0:T(8,128)(2,1)S(1)}, bf16[256,1024]{1,0:T(8,128)(2,1)}, u32[]{:S(2)}) copy-start(bf16[256,1024]{1,0:T(8,128)(2,1)} %param.15) | copy-start | bytes 1572868
  47.5 102.1 %copy-start.12 = (s32[256]{0:T(256)S(1)}, s32[256]{0:T(256)}, u32[]{:S(2)}) copy-start(s32[256]{0:T(256)} %param.17) | copy-start | bytes 3076
  54.6 94.9 %collective-permute-start = (bf16[1024,2048]{0,1:T(8,128)(2,1)S(1)}, bf16[1024,2048]{0,1:T(8,128)(2,1)}, u32[]{:S(2)}, u32[]{:S(2)}) collective-permute-start(bf16[1024,2048]{0,1:T(8,128)(2,1)S(1)} %get-tuple-element.207), channel_id=1, source_target_pairs={{0,64},{1,65},{2,66},{3,67},{4,68},{5,69},{6,70},{7,71},{8,72},{9,... | collective-permute-start | bytes 12582920 | tf_op jit(solution)/shard_map/ppermute | solution.py:14
  149.7 7.8 %copy-start.1 = (bf16[256,4096]{1,0:T(8,128)(2,1)}, bf16[256,4096]{1,0:T(8,128)(2,1)S(1)}, u32[]{:S(2)}) copy-start(bf16[256,4096]{1,0:T(8,128)(2,1)S(1)} %get-tuple-element.192) | copy-start | bytes 6291460 | tf_op jit(solution)/shard_map/cond
  226.1 3.4 slice-start
  229.1 2.3 slice-start.1
  229.1 2.3 copy-start.9
  231.5 2.4 copy-start.2
  242.0 89.8 %copy-start.5 = (bf16[256,4096]{1,0:T(8,128)(2,1)}, bf16[256,4096]{1,0:T(8,128)(2,1)S(1)}, u32[]{:S(2)}) copy-start(bf16[256,4096]{1,0:T(8,128)(2,1)S(1)} %get-tuple-element.208) | copy-start | bytes 6291460
  242.0 89.8 %collective-permute-start.1 = (bf16[1024,2048]{1,0:T(8,128)(2,1)S(1)}, bf16[1024,2048]{1,0:T(8,128)(2,1)S(1)}, u32[]{:S(2)}, u32[]{:S(2)}) collective-permute-start(bf16[1024,2048]{1,0:T(8,128)(2,1)S(1)} %get-tuple-element.210), channel_id=1, source_target_pairs={{64,0},{65,1},{66,2},{67,3},{68,4},{69,5},{70,6},{71,7},{72,8},{73... | collective-permute-start | bytes 12582920 | tf_op jit(solution)/shard_map/ppermute | solution.py:14
  349.3 233.0 %reduce-scatter.5.cloned.1.call-start = ((), (), s32[]{:S(2)}) async-start(), calls=%async_computation.3 | async-start | bytes 17825792 | tf_op jit(solution)/shard_map/reduce_scatter | solution.py:162
Sparse Core Ops, SparseCore 0:
  9.7 33.2 all-gather.2
  349.4 49.6 reduce-scatter.2
  402.3 180.0 reduce-scatter.4
where the time goes:
time: 592 us; the launch traced here: 589 us
  waiting for transfers between devices  444 us (75%)
  matrix products  74 us (12%)
  local copies, waits for them, and re-layouts  44.3 us (7%)
  between operations  13.8 us (2%)
  other arithmetic  9.47 us (2%)
    ppermute x2, waiting for transfers between devices, from_behind(): return lax.ppermute(shard, axis, pairs)  182 us
    reduce_scatter x1, waiting for transfers between devices, local(): lax.psum_scatter(weight_part, 'win', scatter_dimension=0, tiled=True)  181 us
    reduce_scatter x1, waiting for transfers between devices, local(): lax.psum_scatter(input_part.astype(jnp.bfloat16), 'mp', scatter_dimension...  49.1 us
    all_gather x1, waiting for transfers between devices, local(): gathered = lax.all_gather(local_rows, 'mp', axis=1, tiled=True)  30.3 us
    another operation x4, local copies, waits for them, and re-layouts  19.4 us
    dot_general x8, matrix products, one_head(): jnp.einsum('qk,qd->kd', rounded, upstream, preferred_element_type=jnp.flo...  16.2 us
  transfers between devices with their start and end apart: 5, of which 5 were waited for; matrix products, arithmetic and copies ran while one was open for 1% of the time, Pallas kernels for 0%

commit v1 on v0

v1 whole, which is shorter than its diff:
```python
import jax
import jax.numpy as jnp
from jax import lax
from jax.experimental import pallas as pl
from jax.experimental.pallas import tpu as pltpu
from jax.sharding import PartitionSpec as P

MESH = pl.DeviceIdType.MESH
BF = jnp.bfloat16
F32 = jnp.float32
FACTOR = 128 ** (-0.5)
BLK = 256
WIDE = 1024
HALF = 128


def nn(a, b):
    return jnp.dot(a, b, preferred_element_type=F32)


def nt(a, b):
    return lax.dot_general(a, b, (((1,), (1,)), ((), ())), preferred_element_type=F32)


def tn(a, b):
    return lax.dot_general(a, b, (((0,), (0,)), ((), ())), preferred_element_type=F32)


def ds(i, size):
    return pl.ds(pl.multiple_of(i * size, size), size)


def rcopy(src, dst, send_sem, recv_sem, device):
    return pltpu.make_async_remote_copy(
        src_ref=src,
        dst_ref=dst,
        send_sem=send_sem,
        recv_sem=recv_sem,
        device_id=device,
        device_id_type=MESH,
    )


def kernel(
    tok, proj, cot, counts, frames, ig, wg,
    TOK, W, COT, ACC, Q, U, BIAS, K, V, S, DP, KG, VG, QG, FT, TOKX, QGX,
    CS, CR, KEEP, X1S, X1R, X2S, X2R, YS, YR, PS, RAL, RAR, RBL, RBR,
    l_sem, ag_s, ag_r, q_s, q_r, qg_s, qg_r, aa_s, aa_r, xg_s, xg_r,
    cs_s, cs_r, x1_s, x1_r, x2_s, x2_r, y_s, y_r, rs_s, rs_r,
):
    g = lax.axis_index("group")
    w = lax.axis_index("win")
    m = lax.axis_index("mp")
    x = w // 4
    yl = (w // 2) % 2
    c = w % 2
    is_video = g == 0
    is_neural = g == 1
    right_m, left_m, far_m = (m + 1) % 4, (m + 3) % 4, (m + 2) % 4
    right, left = {"mp": right_m}, {"mp": left_m}
    partner = {"group": 1 - g}
    core = {"win": w + 1 - 2 * c}
    yside = {"win": w + 2 - 4 * yl}

    def xdev(xp):
        return {"win": xp * 4 + w % 4}

    xnear = xdev(x + 1 - 2 * (x % 2))
    xback = xdev(3 - x)
    keep_kind = ((x + 1) // 2) % 2

    load_tok = pltpu.make_async_copy(tok.at[0], TOK.at[m], l_sem.at[0])
    load_tok.start()
    load_cot = pltpu.make_async_copy(cot, COT, l_sem.at[1])

    def load_w(i, b):
        return pltpu.make_async_copy(proj.at[0, ds(b, WIDE)], W.at[b], l_sem.at[2 + i])

    order = (m, left_m, right_m, far_m)

    @pl.when(is_neural)
    def _():
        for i in range(4):
            load_w(i, order[i]).start()

    @pl.when(is_video)
    def _():
        for i in range(2):
            load_w(i, i).start()

    load_cot.start()

    barrier = pltpu.get_barrier_semaphore()
    greet = [right, left, partner, core, yside] + [xdev((x + d) % 4) for d in (1, 2, 3)]
    for device in greet:
        pl.semaphore_signal(barrier, inc=1, device_id=device, device_id_type=MESH)
    pl.semaphore_wait(barrier, len(greet))

    lo, hi = pl.ds(0, HALF), pl.ds(HALF, HALF)

    def ring(i, block, rows, device):
        return rcopy(TOK.at[block, rows], TOK.at[block, rows], ag_s.at[i], ag_r.at[i], device)

    load_tok.wait()
    ring(0, m, lo, right).start()
    ring(2, m, hi, left).start()
    ring(1, m, hi, right).start()
    ring(3, m, lo, left).start()

    def project(b, i):
        @pl.when(is_video)
        def _():
            if i == 0:
                load_w(0, 0).wait()
                load_w(1, 1).wait()
            rows = ds(b, BLK)
            for j in range(4):
                cols = pl.ds(j * BLK, BLK)
                K[rows, cols] = nn(TOK[b], W[0, :, cols]).astype(BF)
                V[rows, cols] = nn(TOK[b], W[1, :, cols]).astype(BF)
            FT[:, rows] = TOK[b].T

        @pl.when(is_neural)
        def _():
            load_w(i, b).wait()
            for j in range(4):
                cols = pl.ds(j * BLK, BLK)
                part = nn(TOK[b], W[b, :, cols])
                if i == 0:
                    ACC[:, cols] = part
                elif i < 3:
                    ACC[:, cols] += part
                else:
                    Q[j] = (ACC[:, cols] + part).astype(BF)
                    rcopy(Q.at[j], Q.at[j], q_s.at[j], q_r.at[j], partner).start()

    project(m, 0)
    ring(0, left_m, lo, left).wait_recv()
    ring(4, left_m, lo, right).start()
    ring(2, right_m, hi, right).wait_recv()
    ring(5, right_m, hi, left).start()
    ring(1, left_m, hi, left).wait_recv()
    project(left_m, 1)
    ring(3, right_m, lo, right).wait_recv()
    project(right_m, 2)

    @pl.when(is_video)
    def _():
        load_cot.wait()
        live = lax.broadcasted_iota(jnp.int32, (BLK, BLK), 0) < counts[0]
        for j in range(4):
            part = COT[:, pl.ds(j * BLK, BLK)].astype(F32)
            U[j] = jnp.where(live, part, jnp.zeros_like(part)).astype(BF)
        key_frame = lax.broadcasted_iota(jnp.int32, (BLK, BLK), 0) >> 6
        BIAS[...] = jnp.where(key_frame <= frames[...], 0.0, -1e30).astype(F32)

    ring(4, far_m, lo, left).wait_recv()
    ring(5, far_m, hi, right).wait_recv()
    project(far_m, 3)

    def core_send(p, count):
        return rcopy(CS.at[p, pl.ds(0, count)], CR.at[p, pl.ds(0, count)], cs_s.at[p], cs_r.at[p], core)

    def weight_part(p, kinds, rhs):
        for kind in range(kinds):
            for yd in range(2):
                CS[p, kind * 2 + yd] = nn(FT[ds(2 * yd + 1 - c, BLK)], rhs(kind)).astype(BF)
        core_send(p, 2 * kinds).start()
        for kind in range(kinds):
            for yd in range(2):
                KEEP[p, kind * 2 + yd] = nn(FT[ds(2 * yd + c, BLK)], rhs(kind))

    def y_send(p):
        return rcopy(YS.at[p], YR.at[p], y_s.at[p], y_r.at[p], yside)

    def x1_send(p):
        return rcopy(X1S.at[p], X1R.at[p], x1_s.at[p], x1_r.at[p], xnear)

    def x2_send(p):
        return rcopy(X2S.at[p], X2R.at[p], x2_s.at[p], x2_r.at[p], xback)

    def part_send(i):
        src = (
            PS.at[far_m, lo], PS.at[right_m, hi], PS.at[right_m, lo],
            PS.at[far_m, hi], PS.at[left_m, lo], PS.at[left_m, hi],
        )[i]
        dst = (RAL, RBL.at[hi], RBL.at[lo], RAR, RBR.at[lo], RBR.at[hi])[i]
        return rcopy(src, dst, rs_s.at[i], rs_r.at[i], right if i < 3 else left)

    def input_parts(part):
        part(far_m)
        part_send(0).start()
        part_send(3).start()
        part(right_m)
        part_send(1).start()
        part(left_m)
        part_send(4).start()
        part(m)

    def input_forward():
        part_send(0).wait_recv()
        PS[right_m, lo] = (PS[right_m, lo].astype(F32) + RAL[...].astype(F32)).astype(BF)
        part_send(2).start()
        part_send(3).wait_recv()
        PS[left_m, hi] = (PS[left_m, hi].astype(F32) + RAR[...].astype(F32)).astype(BF)
        part_send(5).start()

    def input_total():
        for i in (1, 2, 4, 5):
            part_send(i).wait_recv()
        return PS[m].astype(F32) + RBL[...].astype(F32) + RBR[...].astype(F32)

    def qg_send(p):
        return rcopy(QG.at[p], QGX.at[p, ds(x, BLK)], qg_s.at[p], qg_r.at[p], partner)

    @pl.when(is_video)
    def _():
        def attend(p, hh):
            cols = ds(2 * p + hh, HALF)
            head = pl.ds(hh * HALF, HALF)
            q = Q[p, :, head]
            u = U[p, :, head]
            top = None
            for t in range(4):
                s = nt(K[pl.ds(t * BLK, BLK), cols], q) + BIAS[...]
                S[t] = s
                high = jnp.max(s, axis=0, keepdims=True)
                top = high if top is None else jnp.maximum(top, high)
            total = jnp.zeros_like(top)
            weighted = jnp.zeros_like(top)
            for t in range(4):
                e = jnp.exp((S[t] - top) * FACTOR)
                d = nt(V[pl.ds(t * BLK, BLK), cols], u)
                S[t] = e
                DP[t] = d
                total += jnp.sum(e, axis=0, keepdims=True)
                weighted += jnp.sum(e * d, axis=0, keepdims=True)
            inverse = 1.0 / total
            mean = weighted * inverse
            query_grad = None
            for t in range(4):
                a = S[t] * inverse
                VG[pl.ds(t * BLK, BLK), cols] = nn(a.astype(BF), u).astype(BF)
                sg = (a * (DP[t] - mean) * FACTOR).astype(BF)
                KG[pl.ds(t * BLK, BLK), cols] = nn(sg, q).astype(BF)
                more = tn(sg, K[pl.ds(t * BLK, BLK), cols])
                query_grad = more if query_grad is None else query_grad + more
            QG[p, :, head] = query_grad.astype(BF)

        def stage_x1(p):
            core_send(p, 4).wait_recv()
            for yd in range(2):
                i = (1 - keep_kind) * 2 + yd
                X1S[p, yd] = (KEEP[p, i] + CR[p, i].astype(F32)).astype(BF)
            x1_send(p).start()
            for yd in range(2):
                i = keep_kind * 2 + yd
                KEEP[p, i] = KEEP[p, i] + CR[p, i].astype(F32)

        def stage_x2(p):
            x1_send(p).wait_recv()
            for yd in range(2):
                i = keep_kind * 2 + yd
                total = KEEP[p, i] + X1R[p, yd].astype(F32)
                KEEP[p, i] = total
                X2S[p, yd] = total.astype(BF)

            @pl.when(x >= 2)
            def _():
                x2_send(p).start()

        def stage_y(p):
            @pl.when(x < 2)
            def _():
                x2_send(p).wait_recv()
                i = keep_kind * 2 + 1 - yl
                YS[p] = (KEEP[p, i] + X2R[p, 1 - yl].astype(F32)).astype(BF)
                y_send(p).start()
                i = keep_kind * 2 + yl
                KEEP[p, i] = KEEP[p, i] + X2R[p, yl].astype(F32)

        def step(p, carry):
            rcopy(Q.at[p], Q.at[p], q_s.at[p], q_r.at[p], partner).wait_recv()
            for hh in range(2):
                attend(p, hh)
            qg_send(p).start()
            cols = ds(p, BLK)
            weight_part(p, 2, lambda kind: (KG, VG)[kind][:, cols])

            @pl.when(p >= 1)
            def _():
                stage_x1(p - 1)

            @pl.when(p >= 2)
            def _():
                stage_x2(p - 2)

            @pl.when(p >= 3)
            def _():
                stage_y(p - 3)

            return carry

        lax.fori_loop(0, 4, step, 0)

        def part(d):
            rows = ds(d, BLK)
            for j in range(4):
                out = pl.ds(j * BLK, BLK)
                PS[d, :, out] = (nt(KG[rows], W[0, out]) + nt(VG[rows], W[1, out])).astype(BF)

        input_parts(part)
        stage_x1(3)
        stage_x2(2)
        input_forward()
        stage_y(1)
        stage_x2(3)
        stage_y(2)
        stage_y(3)
        ig[0] = input_total().astype(BF)

        @pl.when(x < 2)
        def _():
            for p in range(4):
                y_send(p).wait_recv()
                wg[0, :, pl.ds(p * BLK, BLK)] = KEEP[p, keep_kind * 2 + yl] + YR[p].astype(F32)

        @pl.when(x >= 2)
        def _():
            wg[...] = jnp.zeros_like(wg)

        for p in range(4):
            qg_send(p).wait_send()
            core_send(p, 4).wait_send()
            x1_send(p).wait_send()

        @pl.when(x >= 2)
        def _():
            for p in range(4):
                x2_send(p).wait_send()

        @pl.when(x < 2)
        def _():
            for p in range(4):
                y_send(p).wait_send()

    @pl.when(is_neural)
    def _():
        def swap_send(d):
            return rcopy(TOK.at[(x + d) % 4], TOKX.at[x], aa_s.at[d - 1], aa_r.at[d - 1], xdev((x + d) % 4))

        def swap_recv(d):
            s = TOKX.at[(x + 4 - d) % 4]
            return rcopy(s, s, aa_s.at[d - 1], aa_r.at[d - 1], xdev((x + d) % 4))

        for d in (1, 3, 2):
            swap_send(d).start()
        FT[:, ds(x, BLK)] = TOK[x].T
        for d in (1, 3, 2):
            swap_recv(d).wait_recv()
            FT[:, ds((x + 4 - d) % 4, BLK)] = TOKX[(x + 4 - d) % 4].T

        def gather_send(p, d):
            s = QGX.at[p, ds(x, BLK)]
            return rcopy(s, s, xg_s.at[p, d - 1], xg_r.at[p, d - 1], xdev((x + d) % 4))

        def gather_recv(p, d):
            s = QGX.at[p, ds((x + 4 - d) % 4, BLK)]
            return rcopy(s, s, xg_s.at[p, d - 1], xg_r.at[p, d - 1], xdev((x + d) % 4))

        def relay(p):
            qg_send(p).wait_recv()
            for d in (1, 3, 2):
                gather_send(p, d).start()

        def chunk(p):
            for d in (1, 3, 2):
                gather_recv(p, d).wait_recv()
            weight_part(p, 1, lambda kind: QGX[p])

        def stage_y(p):
            core_send(p, 2).wait_recv()
            YS[p] = (KEEP[p, 1 - yl] + CR[p, 1 - yl].astype(F32)).astype(BF)
            y_send(p).start()
            KEEP[p, yl] = KEEP[p, yl] + CR[p, yl].astype(F32)

        def part(d):
            for j in range(4):
                out = pl.ds(j * BLK, BLK)
                total = None
                for p in range(4):
                    more = nt(QGX[p, ds(x, BLK)], W[d, out, pl.ds(p * BLK, BLK)])
                    total = more if total is None else total + more
                PS[d, :, out] = total.astype(BF)

        for p in range(4):
            relay(p)
        input_parts(part)
        chunk(0)
        input_forward()
        stage_y(0)
        for p in range(1, 4):
            chunk(p)
            stage_y(p)
        load_cot.wait()
        ig[0] = (input_total() + COT[...].astype(F32)).astype(BF)
        for p in range(4):
            y_send(p).wait_recv()
            wg[0, :, pl.ds(p * BLK, BLK)] = KEEP[p, yl] + YR[p].astype(F32)
        for p in range(4):
            rcopy(Q.at[p], Q.at[p], q_s.at[p], q_r.at[p], partner).wait_send()
            core_send(p, 2).wait_send()
            y_send(p).wait_send()
            for d in (1, 3, 2):
                gather_send(p, d).wait_send()
        for d in (1, 3, 2):
            swap_send(d).wait_send()

    ring(0, m, lo, right).wait_send()
    ring(2, m, hi, left).wait_send()
    ring(1, m, hi, right).wait_send()
    ring(3, m, lo, left).wait_send()
    ring(4, left_m, lo, right).wait_send()
    ring(5, right_m, hi, left).wait_send()
    for i in range(6):
        part_send(i).wait_send()


def local(tokens, proj, cotangent, counts, frames):
    vmem = pltpu.VMEM
    dma = pltpu.SemaphoreType.DMA
    scratch = [
        vmem((4, BLK, WIDE), BF),
        vmem((4, WIDE, WIDE), BF),
        vmem((BLK, WIDE), BF),
        vmem((BLK, WIDE), F32),
        vmem((4, BLK, BLK), BF),
        vmem((4, BLK, BLK), BF),
        vmem((BLK, BLK), F32),
        vmem((WIDE, WIDE), BF),
        vmem((WIDE, WIDE), BF),
        vmem((4, BLK, BLK), F32),
        vmem((4, BLK, BLK), F32),
        vmem((WIDE, WIDE), BF),
        vmem((WIDE, WIDE), BF),
        vmem((4, BLK, BLK), BF),
        vmem((WIDE, WIDE), BF),
        vmem((4, BLK, WIDE), BF),
        vmem((4, WIDE, BLK), BF),
        vmem((4, 4, BLK, BLK), BF),
        vmem((4, 4, BLK, BLK), BF),
        vmem((4, 4, BLK, BLK), F32),
        vmem((4, 2, BLK, BLK), BF),
        vmem((4, 2, BLK, BLK), BF),
        vmem((4, 2, BLK, BLK), BF),
        vmem((4, 2, BLK, BLK), BF),
        vmem((4, BLK, BLK), BF),
        vmem((4, BLK, BLK), BF),
        vmem((4, BLK, WIDE), BF),
        vmem((HALF, WIDE), BF),
        vmem((HALF, WIDE), BF),
        vmem((BLK, WIDE), BF),
        vmem((BLK, WIDE), BF),
        dma((6,)),
        dma((6,)), dma((6,)),
        dma((4,)), dma((4,)),
        dma((4,)), dma((4,)),
        dma((3,)), dma((3,)),
        dma((4, 3)), dma((4, 3)),
        dma((4,)), dma((4,)),
        dma((4,)), dma((4,)),
        dma((4,)), dma((4,)),
        dma((4,)), dma((4,)),
        dma((6,)), dma((6,)),
    ]
    anywhere = pl.BlockSpec(memory_space=pl.ANY)
    in_vmem = pl.BlockSpec(memory_space=vmem)
    return pl.pallas_call(
        kernel,
        out_shape=(
            jax.ShapeDtypeStruct((1, BLK, WIDE), BF),
            jax.ShapeDtypeStruct((1, BLK, WIDE), F32),
        ),
        in_specs=[
            anywhere, anywhere, anywhere,
            pl.BlockSpec(memory_space=pltpu.SMEM),
            in_vmem,
        ],
        out_specs=(in_vmem, in_vmem),
        scratch_shapes=scratch,
        compiler_params=pltpu.CompilerParams(
            collective_id=0, has_side_effects=True, vmem_limit_bytes=60 * 2**20
        ),
        cost_estimate=pl.CostEstimate(
            flops=20 * 10**9, bytes_accessed=16 * 2**20, transcendentals=2**21
        ),
    )(tokens, proj, cotangent, counts, frames.reshape(1, BLK))


def solution(mesh):
    return jax.shard_map(
        local,
        mesh=mesh,
        in_specs=(
            P("group", "win", "mp"),
            P("group", None, "mp"),
            P("win", "mp"),
            P("win"),
            P("win"),
        ),
        out_specs=(P("group", "win", "mp"), P("group", "win", "mp")),
        check_vma=False,
    )
```

time: 592 us -> 89.3 us (0.15)
  waiting for transfers between devices: 444 us -> 0 us
  Pallas kernels: 0 us -> 83.6 us
  matrix products: 74 us -> 0 us
  local copies, waits for them, and re-layouts: 44.3 us -> 4.17 us
  between operations: 13.8 us -> 1.29 us
  other arithmetic: 9.47 us -> 0 us
    reduce_scatter x2 -> x0, waiting for transfers between devices: 230 us -> none  [the longest x1 181 us: local(): lax.psum_scatter(weight_part, 'win', scatter_dimension=0, tiled=True)]
    ppermute x2 -> x0, waiting for transfers between devices: 182 us -> none  [from_behind(): return lax.ppermute(shard, axis, pairs)]
    pallas_call x0 -> x1, Pallas kernels: none -> 83.6 us  [local(): pl.pallas_call(kernel, out_shape=(jax.ShapeDtypeStruct((1, BLK, WIDE), BF...]
    dot_general x43 -> x0, matrix products: 74 us -> none  [the longest x8 16.2 us: one_head(): jnp.einsum('qk,qd->kd', rounded, upstream, preferred_element_type=jnp.flo...]
    all_gather x1 -> x0, waiting for transfers between devices: 30.3 us -> none  [local(): gathered = lax.all_gather(local_rows, 'mp', axis=1, tiled=True)]
    another operation x4 -> x0, local copies, waits for them, and re-layouts: 19.4 us -> none
    slice x2 -> x0, local copies, waits for them, and re-layouts: 9.47 us -> none  [the longest x1 4.75 us: local(): w_value = weight[DV:2 * DV]]
    reshape x2 -> x0, local copies, waits for them, and re-layouts: 7.48 us -> none  [the longest x1 4.49 us: local(): features = gathered.reshape(video_rows, DV)]
  transfers between devices with their start and end apart: 5 -> 0, of which waited for: 5 -> 0; matrix products, arithmetic and copies ran while one was open for 1% -> 0% of each run, Pallas kernels for 0% -> 0%
where the time goes in v1:
time: 89.3 us; the launch traced here: 89 us
  Pallas kernels  83.6 us (94%)
  local copies, waits for them, and re-layouts  4.17 us (5%)
  between operations  1.29 us (1%)
    pallas_call x1, Pallas kernels, local(): pl.pallas_call(kernel, out_shape=(jax.ShapeDtypeStruct((1, BLK, WIDE), BF...  83.6 us
    unnamed x2, local copies, waits for them, and re-layouts  4.17 us

profile of v1, /device:TPU:17, one launch (start us, length us, event | category | flops | bytes accessed | tf_op | source)
XLA Modules:
  0.0 89.0 jit_solution(2521649376146559599)
XLA Ops:
  1.3 83.6 %shard_map.68 = (bf16[1,256,1024]{2,1,0:T(8,128)(2,1)}, f32[1,256,1024]{2,1,0:T(8,128)}) custom-call(bf16[1,256,1024]{2,1,0:T(8,128)(2,1)} %tok.1, bf16[1,4096,1024]{2,1,0:T(8,128)(2,1)} %proj.1, bf16[256,1024]{1,0:T(8,128)(2,1)} %cot.1, s32[1]{0:T(128)S(6)} %copy.9.counts, s32[1,256]{1,0:T(1,128)} %bitcast.1), custom_call_target="tpu_custom_call" | custom-call | flops 20000000000 | bytes 16777216 | tf_op jit(solution)/shard_map/pallas_call | solution.py:478
  84.9 1.9 %copy.10 = bf16[1,256,1024]{2,1,0:T(8,128)(2,1)} copy(bf16[1,256,1024]{2,1,0:T(8,128)(2,1)} %get-tuple-element.4) | data formatting | bytes 1048576
  86.7 2.3 %copy.11 = f32[1,256,1024]{2,1,0:T(8,128)} copy(f32[1,256,1024]{2,1,0:T(8,128)} %get-tuple-element.5) | data formatting | bytes 2097152

commit v2 on v1

v2 whole, which is shorter than its diff:
```python
import jax
import jax.numpy as jnp
from jax import lax
from jax.experimental import pallas as pl
from jax.experimental.pallas import tpu as pltpu
from jax.sharding import PartitionSpec as P

MESH = pl.DeviceIdType.MESH
BF = jnp.bfloat16
F32 = jnp.float32
FACTOR = 128 ** (-0.5)
LOG2_E = 1.4426950408889634
BLK = 256
WIDE = 1024
HALF = 128
PIECE = 64


def nn(a, b):
    return jnp.dot(a, b, preferred_element_type=F32)


def nt(a, b):
    return lax.dot_general(a, b, (((1,), (1,)), ((), ())), preferred_element_type=F32)


def tn(a, b):
    return lax.dot_general(a, b, (((0,), (0,)), ((), ())), preferred_element_type=F32)


def ds(i, size):
    return pl.ds(pl.multiple_of(i * size, size), size)


def rcopy(src, dst, send_sem, recv_sem, device):
    return pltpu.make_async_remote_copy(
        src_ref=src,
        dst_ref=dst,
        send_sem=send_sem,
        recv_sem=recv_sem,
        device_id=device,
        device_id_type=MESH,
    )


def kernel(
    tok, proj, cot, counts, frames, ig, wg,
    TOK, W, COT, ACC, Q, U, BIAS, K, KT, V, S, DP, KG, VG, QG, FT, TOKX, QGX,
    CS, CR, KEEP, X1S, X1R, X2S, X2R, YS, YR, ZS, ZR, PS, RAL, RAR, RBL, RBR,
    l_sem, ag_s, ag_r, q_s, q_r, qg_s, qg_r, aa_s, aa_r, ar_s, ar_r, xg_s, xg_r,
    cs_s, cs_r, x1_s, x1_r, x2_s, x2_r, y_s, y_r, z_s, z_r, rs_s, rs_r,
):
    g = lax.axis_index("group")
    w = lax.axis_index("win")
    m = lax.axis_index("mp")
    x = w // 4
    yl = (w // 2) % 2
    c = w % 2
    is_video = g == 0
    is_neural = g == 1
    right_m, left_m, far_m = (m + 1) % 4, (m + 3) % 4, (m + 2) % 4
    right, left = {"mp": right_m}, {"mp": left_m}
    partner = {"group": 1 - g}
    core = {"win": w + 1 - 2 * c}
    yside = {"win": w + 2 - 4 * yl}

    def xdev(xp):
        return {"win": xp * 4 + w % 4}

    xnear = xdev(x + 1 - 2 * (x % 2))
    xback = xdev(3 - x)
    keep_kind = ((x + 1) // 2) % 2

    load_tok = pltpu.make_async_copy(tok.at[0], TOK.at[m], l_sem.at[0])
    load_tok.start()
    load_cot = pltpu.make_async_copy(cot, COT, l_sem.at[1])

    def load_w(i, b):
        return pltpu.make_async_copy(proj.at[0, ds(b, WIDE)], W.at[b], l_sem.at[2 + i])

    order = (m, left_m, right_m, far_m)

    @pl.when(is_neural)
    def _():
        for i in range(4):
            load_w(i, order[i]).start()

    @pl.when(is_video)
    def _():
        for i in range(2):
            load_w(i, i).start()

    load_cot.start()

    barrier = pltpu.get_barrier_semaphore()
    greet = [right, left, partner, core, yside] + [xdev((x + d) % 4) for d in (1, 2, 3)]
    for device in greet:
        pl.semaphore_signal(barrier, inc=1, device_id=device, device_id_type=MESH)
    pl.semaphore_wait(barrier, len(greet))

    lo, hi = pl.ds(0, HALF), pl.ds(HALF, HALF)

    def ring(half, i, block):
        device = right if i in (0, 1, 4) else left
        start = half * HALF + (0 if i in (0, 3, 4) else PIECE)
        rows = pl.ds(start, PIECE)
        return rcopy(TOK.at[block, rows], TOK.at[block, rows], ag_s.at[half, i], ag_r.at[half, i], device)

    def ring_start(half):
        for i in (0, 2, 1, 3):
            ring(half, i, m).start()

    def ring_forward(half):
        ring(half, 0, left_m).wait_recv()
        ring(half, 4, left_m).start()
        ring(half, 2, right_m).wait_recv()
        ring(half, 5, right_m).start()

    def q_send(j, half):
        s = Q.at[j, pl.ds(half * HALF, HALF)]
        return rcopy(s, s, q_s.at[j, half], q_r.at[j, half], partner)

    def project(b, i, half):
        rows = pl.ds(half * HALF, HALF)

        @pl.when(is_video)
        def _():
            if i == 0 and half == 0:
                load_w(0, 0).wait()
                load_w(1, 1).wait()
            keys = ds(2 * b + half, HALF)
            for j in range(4):
                cols = pl.ds(j * BLK, BLK)
                K[keys, cols] = nn(TOK[b, rows], W[0, :, cols]).astype(BF)
                V[keys, cols] = nn(TOK[b, rows], W[1, :, cols]).astype(BF)
            FT[:, keys] = TOK[b, rows].T
            KT[:, keys] = K[keys].T

        @pl.when(is_neural)
        def _():
            if half == 0:
                load_w(i, b).wait()
            for j in range(4):
                cols = pl.ds(j * BLK, BLK)
                part = nn(TOK[b, rows], W[b, :, cols])
                if i == 0:
                    ACC[rows, cols] = part
                elif i < 3:
                    ACC[rows, cols] += part
                else:
                    Q[j, rows] = (ACC[rows, cols] + part).astype(BF)
                    q_send(j, half).start()

    eighth = HALF // 4

    def swap_send(half, d):
        rows = ds(4 * half + m, eighth)
        return rcopy(
            TOK.at[(x + d) % 4, rows], TOKX.at[x, rows],
            aa_s.at[half, d - 1], aa_r.at[half, d - 1], xdev((x + d) % 4),
        )

    def swap_recv(half, d):
        s = TOKX.at[(x + 4 - d) % 4, ds(4 * half + m, eighth)]
        return rcopy(s, s, aa_s.at[half, d - 1], aa_r.at[half, d - 1], xdev((x + d) % 4))

    load_tok.wait()
    ring_start(0)
    project(m, 0, 0)
    ring_forward(0)
    ring_start(1)
    ring(0, 1, left_m).wait_recv()
    project(left_m, 1, 0)
    ring(0, 3, right_m).wait_recv()
    project(right_m, 2, 0)
    ring(0, 4, far_m).wait_recv()
    ring(0, 5, far_m).wait_recv()
    project(far_m, 3, 0)

    @pl.when(is_neural)
    def _():
        for d in (1, 3, 2):
            swap_send(0, d).start()

    project(m, 0, 1)
    ring_forward(1)
    ring(1, 1, left_m).wait_recv()
    project(left_m, 1, 1)
    ring(1, 3, right_m).wait_recv()
    project(right_m, 2, 1)

    @pl.when(is_video)
    def _():
        load_cot.wait()
        live = lax.broadcasted_iota(jnp.int32, (BLK, BLK), 0) < counts[0]
        for j in range(4):
            part = COT[:, pl.ds(j * BLK, BLK)].astype(F32)
            U[j] = jnp.where(live, part, jnp.zeros_like(part)).astype(BF)
        key_frame = lax.broadcasted_iota(jnp.int32, (BLK, BLK), 0) >> 6
        BIAS[...] = jnp.where(key_frame <= frames[...], 0.0, -1e30).astype(F32)

    ring(1, 4, far_m).wait_recv()
    ring(1, 5, far_m).wait_recv()
    project(far_m, 3, 1)

    def core_send(p, count):
        return rcopy(CS.at[p, pl.ds(0, count)], CR.at[p, pl.ds(0, count)], cs_s.at[p], cs_r.at[p], core)

    def weight_part(p, kinds, rhs):
        for kind in range(kinds):
            for yd in range(2):
                CS[p, kind * 2 + yd] = nn(FT[ds(2 * yd + 1 - c, BLK)], rhs(kind)).astype(BF)
        core_send(p, 2 * kinds).start()
        for kind in range(kinds):
            for yd in range(2):
                KEEP[p, kind * 2 + yd] = nn(FT[ds(2 * yd + c, BLK)], rhs(kind))

    def y_send(p):
        return rcopy(YS.at[p], YR.at[p], y_s.at[p], y_r.at[p], yside)

    def x1_send(p, n):
        some = pl.ds(0, n)
        return rcopy(X1S.at[p, some], X1R.at[p, some], x1_s.at[p], x1_r.at[p], xnear)

    def x2_send(p, n):
        some = pl.ds(0, n)
        return rcopy(X2S.at[p, some], X2R.at[p, some], x2_s.at[p], x2_r.at[p], xback)

    def part_send(i):
        src = (
            PS.at[far_m, lo], PS.at[right_m, hi], PS.at[right_m, lo],
            PS.at[far_m, hi], PS.at[left_m, lo], PS.at[left_m, hi],
        )[i]
        dst = (RAL, RBL.at[hi], RBL.at[lo], RAR, RBR.at[lo], RBR.at[hi])[i]
        return rcopy(src, dst, rs_s.at[i], rs_r.at[i], right if i < 3 else left)

    def input_parts(part, first, second, third):
        part(far_m)
        part_send(0).start()
        part_send(3).start()
        first()
        part(right_m)
        part_send(1).start()
        part(left_m)
        part_send(4).start()
        second()
        part(m)
        third()

    def input_forward():
        part_send(0).wait_recv()
        PS[right_m, lo] = (PS[right_m, lo].astype(F32) + RAL[...].astype(F32)).astype(BF)
        part_send(2).start()
        part_send(3).wait_recv()
        PS[left_m, hi] = (PS[left_m, hi].astype(F32) + RAR[...].astype(F32)).astype(BF)
        part_send(5).start()

    def input_total():
        for i in (1, 2, 4, 5):
            part_send(i).wait_recv()
        return PS[m].astype(F32) + RBL[...].astype(F32) + RBR[...].astype(F32)

    def qg_send(p):
        return rcopy(QG.at[p], QGX.at[p, ds(x, BLK)], qg_s.at[p], qg_r.at[p], partner)

    @pl.when(is_video)
    def _():
        def attend(p):
            blocks = [pl.ds(t * BLK, BLK) for t in range(4)]

            def scores(hh):
                cols = ds(2 * p + hh, HALF)
                head = pl.ds(hh * HALF, HALF)
                q = Q[p, :, head]
                u = U[p, :, head]
                q_t = q.T
                top = None
                for t in range(4):
                    s = nn(K[blocks[t], cols], q_t) + BIAS[...]
                    S[4 * hh + t] = s
                    high = jnp.max(s, axis=0, keepdims=True)
                    top = high if top is None else jnp.maximum(top, high)
                return cols, head, q, u, top

            def weights(hh, cols, u, top):
                u_t = u.T
                total = jnp.zeros_like(top)
                weighted = jnp.zeros_like(top)
                for t in range(4):
                    e = jnp.exp2((S[4 * hh + t] - top) * (FACTOR * LOG2_E))
                    d = nn(V[blocks[t], cols], u_t)
                    S[4 * hh + t] = e
                    DP[4 * hh + t] = d
                    total += jnp.sum(e, axis=0, keepdims=True)
                    weighted += jnp.sum(e * d, axis=0, keepdims=True)
                inverse = 1.0 / total
                return inverse, weighted * inverse

            def grads(hh, cols, head, q, u, inverse, mean):
                query_grad = None
                for t in range(4):
                    a = S[4 * hh + t] * inverse
                    VG[blocks[t], cols] = nn(a.astype(BF), u).astype(BF)
                    sg = (a * (DP[4 * hh + t] - mean) * FACTOR).astype(BF)
                    KG[blocks[t], cols] = nn(sg, q).astype(BF)
                    more = nn(KT[cols, blocks[t]], sg)
                    query_grad = more if query_grad is None else query_grad + more
                QG[p, :, head] = query_grad.T.astype(BF)

            cols0, head0, q0, u0, top0 = scores(0)
            inverse0, mean0 = weights(0, cols0, u0, top0)
            cols1, head1, q1, u1, top1 = scores(1)
            grads(0, cols0, head0, q0, u0, inverse0, mean0)
            inverse1, mean1 = weights(1, cols1, u1, top1)
            grads(1, cols1, head1, q1, u1, inverse1, mean1)

        def fold(p, i):
            return KEEP[p, i] + CR[p, i].astype(F32)

        def far_kind(yd):
            return (1 - keep_kind) * 2 + yd

        def near_kind(yd):
            return keep_kind * 2 + yd

        def x1_early(p):
            core_send(p, 4).wait_recv()
            for yd in range(2):
                X1S[p, yd] = fold(p, far_kind(yd)).astype(BF)
            x1_send(p, 2).start()
            for yd in range(2):
                KEEP[p, near_kind(yd)] = fold(p, near_kind(yd))

        def x2_early(p):
            x1_send(p, 2).wait_recv()
            for yd in range(2):
                total = KEEP[p, near_kind(yd)] + X1R[p, yd].astype(F32)
                KEEP[p, near_kind(yd)] = total
                X2S[p, yd] = total.astype(BF)

            @pl.when(x >= 2)
            def _():
                x2_send(p, 2).start()

        def y_early(p):
            @pl.when(x < 2)
            def _():
                x2_send(p, 2).wait_recv()
                YS[p] = (KEEP[p, near_kind(1 - yl)] + X2R[p, 1 - yl].astype(F32)).astype(BF)
                y_send(p).start()
                KEEP[p, near_kind(yl)] = KEEP[p, near_kind(yl)] + X2R[p, yl].astype(F32)

        def z_send(p):
            return rcopy(ZS.at[p - 2], ZR.at[p - 2], z_s.at[p - 2], z_r.at[p - 2], yside)

        def y_late(p):
            core_send(p, 4).wait_recv()
            for kind in range(2):
                ZS[p - 2, kind] = fold(p, 2 * kind + 1 - yl).astype(BF)
            z_send(p).start()
            for kind in range(2):
                KEEP[p, 2 * kind + yl] = fold(p, 2 * kind + yl)

        def x1_late(p):
            z_send(p).wait_recv()
            far = 1 - keep_kind
            X1S[p, 0] = (KEEP[p, far_kind(yl)] + ZR[p - 2, far].astype(F32)).astype(BF)
            x1_send(p, 1).start()
            KEEP[p, near_kind(yl)] = KEEP[p, near_kind(yl)] + ZR[p - 2, keep_kind].astype(F32)

        def x2_late(p):
            x1_send(p, 1).wait_recv()
            total = KEEP[p, near_kind(yl)] + X1R[p, 0].astype(F32)
            KEEP[p, near_kind(yl)] = total
            X2S[p, 0] = total.astype(BF)

            @pl.when(x >= 2)
            def _():
                x2_send(p, 1).start()

        def pair(p):
            for half in range(2):
                q_send(p, half).wait_recv()
            attend(p)
            qg_send(p).start()

        def weigh(p):
            cols = ds(p, BLK)
            weight_part(p, 2, lambda kind: (KG, VG)[kind][:, cols])

        def early_step(p, carry):
            pair(p)

            @pl.when(p == 1)
            def _():
                x1_early(0)

            weigh(p)
            return carry

        def late_step(p, carry):
            pair(p)

            @pl.when(p == 2)
            def _():
                x1_early(1)

            return carry

        lax.fori_loop(0, 2, early_step, 0)
        lax.fori_loop(2, 4, late_step, 0)

        def part(d):
            rows = ds(d, BLK)
            for j in range(4):
                out = pl.ds(j * BLK, BLK)
                PS[d, :, out] = (nt(KG[rows], W[0, out]) + nt(VG[rows], W[1, out])).astype(BF)

        def first():
            weigh(2)
            x2_early(0)
            weigh(3)
            y_late(2)

        input_parts(part, first, lambda: y_late(3), lambda: x2_early(1))
        input_forward()
        y_early(0)
        x1_late(2)
        y_early(1)
        x1_late(3)
        x2_late(2)
        x2_late(3)
        ig[0] = input_total().astype(BF)

        @pl.when(x < 2)
        def _():
            for p in range(2):
                y_send(p).wait_recv()
                wg[0, :, pl.ds(p * BLK, BLK)] = KEEP[p, near_kind(yl)] + YR[p].astype(F32)
            for p in range(2, 4):
                x2_send(p, 1).wait_recv()
                wg[0, :, pl.ds(p * BLK, BLK)] = KEEP[p, near_kind(yl)] + X2R[p, 0].astype(F32)

        @pl.when(x >= 2)
        def _():
            wg[...] = jnp.zeros_like(wg)

        for p in range(4):
            n = 2 if p < 2 else 1
            qg_send(p).wait_send()
            core_send(p, 4).wait_send()
            x1_send(p, n).wait_send()
            if p >= 2:
                z_send(p).wait_send()

        @pl.when(x >= 2)
        def _():
            for p in range(4):
                x2_send(p, 2 if p < 2 else 1).wait_send()

        @pl.when(x < 2)
        def _():
            for p in range(2):
                y_send(p).wait_send()

    @pl.when(is_neural)
    def _():
        tiny = eighth // 2

        def spread(half, d, i, rows):
            s = TOKX.at[(x + 4 - d) % 4, rows]
            device = right if i % 2 == 0 else left
            return rcopy(s, s, ar_s.at[half, d - 1, i], ar_r.at[half, d - 1, i], device)

        def eighth_of(half, b):
            return ds(4 * half + b, eighth)

        def first_of(half, b):
            return ds(8 * half + 2 * b, tiny)

        def second_of(half, b):
            return ds(8 * half + 2 * b + 1, tiny)

        def spread_start(half):
            for d in (1, 3, 2):
                swap_recv(half, d).wait_recv()
                spread(half, d, 0, eighth_of(half, m)).start()
                spread(half, d, 1, eighth_of(half, m)).start()

        def spread_on(half):
            for d in (1, 3, 2):
                spread(half, d, 0, eighth_of(half, left_m)).wait_recv()
                spread(half, d, 2, first_of(half, left_m)).start()
                spread(half, d, 1, eighth_of(half, right_m)).wait_recv()
                spread(half, d, 3, second_of(half, right_m)).start()

        def spread_end():
            for d in (1, 3, 2):
                for half in range(2):
                    spread(half, d, 2, first_of(half, far_m)).wait_recv()
                    spread(half, d, 3, second_of(half, far_m)).wait_recv()
                FT[:, ds((x + 4 - d) % 4, BLK)] = TOKX[(x + 4 - d) % 4].T

        right_x, left_x, far_x = (x + 1) % 4, (x + 3) % 4, (x + 2) % 4

        def gather(p, i, block):
            rows = (ds(block, BLK), ds(block, BLK), ds(2 * block, HALF), ds(2 * block + 1, HALF))[i]
            s = QGX.at[p, rows]
            return rcopy(s, s, xg_s.at[p, i], xg_r.at[p, i], xdev(right_x if i % 2 == 0 else left_x))

        def relay(p):
            qg_send(p).wait_recv()
            gather(p, 0, x).start()
            gather(p, 1, x).start()

        def relay_on(p):
            gather(p, 0, left_x).wait_recv()
            gather(p, 2, left_x).start()
            gather(p, 1, right_x).wait_recv()
            gather(p, 3, right_x).start()

        def chunk(p):
            gather(p, 2, far_x).wait_recv()
            gather(p, 3, far_x).wait_recv()
            weight_part(p, 1, lambda kind: QGX[p])

        def stage_y(p):
            core_send(p, 2).wait_recv()
            YS[p] = (KEEP[p, 1 - yl] + CR[p, 1 - yl].astype(F32)).astype(BF)
            y_send(p).start()
            KEEP[p, yl] = KEEP[p, yl] + CR[p, yl].astype(F32)

        def part(d):
            for j in range(4):
                out = pl.ds(j * BLK, BLK)
                total = None
                for p in range(4):
                    more = nt(QGX[p, ds(x, BLK)], W[d, out, pl.ds(p * BLK, BLK)])
                    total = more if total is None else total + more
                PS[d, :, out] = total.astype(BF)

        for d in (1, 3, 2):
            swap_send(1, d).start()
        spread_start(0)
        FT[:, ds(x, BLK)] = TOK[x].T
        spread_start(1)
        spread_on(0)
        relay(0)
        spread_on(1)
        relay(1)
        relay_on(0)
        relay(2)
        relay_on(1)
        relay(3)

        def third():
            relay_on(3)
            spread_end()
            chunk(0)

        input_parts(part, lambda: relay_on(2), lambda: None, third)
        input_forward()
        stage_y(0)
        for p in range(1, 4):
            chunk(p)
            stage_y(p)
        load_cot.wait()
        ig[0] = (input_total() + COT[...].astype(F32)).astype(BF)
        for p in range(4):
            y_send(p).wait_recv()
            wg[0, :, pl.ds(p * BLK, BLK)] = KEEP[p, yl] + YR[p].astype(F32)
        for p in range(4):
            core_send(p, 2).wait_send()
            y_send(p).wait_send()
            gather(p, 0, x).wait_send()
            gather(p, 1, x).wait_send()
            gather(p, 2, left_x).wait_send()
            gather(p, 3, right_x).wait_send()
            for half in range(2):
                q_send(p, half).wait_send()
        for half in range(2):
            for d in (1, 3, 2):
                swap_send(half, d).wait_send()
                spread(half, d, 0, eighth_of(half, m)).wait_send()
                spread(half, d, 1, eighth_of(half, m)).wait_send()
                spread(half, d, 2, first_of(half, left_m)).wait_send()
                spread(half, d, 3, second_of(half, right_m)).wait_send()

    for half in range(2):
        for i in range(4):
            ring(half, i, m).wait_send()
        ring(half, 4, left_m).wait_send()
        ring(half, 5, right_m).wait_send()
    for i in range(6):
        part_send(i).wait_send()


def local(tokens, proj, cotangent, counts, frames):
    vmem = pltpu.VMEM
    dma = pltpu.SemaphoreType.DMA
    scratch = [
        vmem((4, BLK, WIDE), BF),
        vmem((4, WIDE, WIDE), BF),
        vmem((BLK, WIDE), BF),
        vmem((BLK, WIDE), F32),
        vmem((4, BLK, BLK), BF),
        vmem((4, BLK, BLK), BF),
        vmem((BLK, BLK), F32),
        vmem((WIDE, WIDE), BF),
        vmem((WIDE, WIDE), BF),
        vmem((WIDE, WIDE), BF),
        vmem((8, BLK, BLK), F32),
        vmem((8, BLK, BLK), F32),
        vmem((WIDE, WIDE), BF),
        vmem((WIDE, WIDE), BF),
        vmem((4, BLK, BLK), BF),
        vmem((WIDE, WIDE), BF),
        vmem((4, BLK, WIDE), BF),
        vmem((4, WIDE, BLK), BF),
        vmem((4, 4, BLK, BLK), BF),
        vmem((4, 4, BLK, BLK), BF),
        vmem((4, 4, BLK, BLK), F32),
        vmem((4, 2, BLK, BLK), BF),
        vmem((4, 2, BLK, BLK), BF),
        vmem((4, 2, BLK, BLK), BF),
        vmem((4, 2, BLK, BLK), BF),
        vmem((4, BLK, BLK), BF),
        vmem((4, BLK, BLK), BF),
        vmem((2, 2, BLK, BLK), BF),
        vmem((2, 2, BLK, BLK), BF),
        vmem((4, BLK, WIDE), BF),
        vmem((HALF, WIDE), BF),
        vmem((HALF, WIDE), BF),
        vmem((BLK, WIDE), BF),
        vmem((BLK, WIDE), BF),
        dma((6,)),
        dma((2, 6)), dma((2, 6)),
        dma((4, 2)), dma((4, 2)),
        dma((4,)), dma((4,)),
        dma((2, 3)), dma((2, 3)),
        dma((2, 3, 4)), dma((2, 3, 4)),
        dma((4, 4)), dma((4, 4)),
        dma((4,)), dma((4,)),
        dma((4,)), dma((4,)),
        dma((4,)), dma((4,)),
        dma((4,)), dma((4,)),
        dma((2,)), dma((2,)),
        dma((6,)), dma((6,)),
    ]
    anywhere = pl.BlockSpec(memory_space=pl.ANY)
    in_vmem = pl.BlockSpec(memory_space=vmem)
    return pl.pallas_call(
        kernel,
        out_shape=(
            jax.ShapeDtypeStruct((1, BLK, WIDE), BF),
            jax.ShapeDtypeStruct((1, BLK, WIDE), F32),
        ),
        in_specs=[
            anywhere, anywhere, anywhere,
            pl.BlockSpec(memory_space=pltpu.SMEM),
            in_vmem,
        ],
        out_specs=(in_vmem, in_vmem),
        scratch_shapes=scratch,
        compiler_params=pltpu.CompilerParams(
            collective_id=0, has_side_effects=True, vmem_limit_bytes=60 * 2**20
        ),
        cost_estimate=pl.CostEstimate(
            flops=20 * 10**9, bytes_accessed=16 * 2**20, transcendentals=2**21
        ),
    )(tokens, proj, cotangent, counts, frames.reshape(1, BLK))


def solution(mesh):
    return jax.shard_map(
        local,
        mesh=mesh,
        in_specs=(
            P("group", "win", "mp"),
            P("group", None, "mp"),
            P("win", "mp"),
            P("win"),
            P("win"),
        ),
        out_specs=(P("group", "win", "mp"), P("group", "win", "mp")),
        check_vma=False,
    )
```

time: 89.3 us -> 78.7 us (0.88)
  Pallas kernels: 83.6 us -> 73 us
    pallas_call x1, Pallas kernels: 83.6 us -> 73 us  [local(): pl.pallas_call(kernel, out_shape=(jax.ShapeDtypeStruct((1, BLK, WIDE), BF...]
where the time goes in v2:
time: 78.7 us; the launch traced here: 78.5 us
  Pallas kernels  73 us (93%)
  local copies, waits for them, and re-layouts  4.17 us (5%)
  between operations  1.29 us (2%)
    pallas_call x1, Pallas kernels, local(): pl.pallas_call(kernel, out_shape=(jax.ShapeDtypeStruct((1, BLK, WIDE), BF...  73 us
    unnamed x2, local copies, waits for them, and re-layouts  4.17 us

profile of v2, /device:TPU:17, one launch (start us, length us, event | category | flops | bytes accessed | tf_op | source)
XLA Modules:
  0.0 78.5 jit_solution(886653202543990554)
XLA Ops:
  1.3 73.0 %shard_map.68 = (bf16[1,256,1024]{2,1,0:T(8,128)(2,1)}, f32[1,256,1024]{2,1,0:T(8,128)}) custom-call(bf16[1,256,1024]{2,1,0:T(8,128)(2,1)} %tok.1, bf16[1,4096,1024]{2,1,0:T(8,128)(2,1)} %proj.1, bf16[256,1024]{1,0:T(8,128)(2,1)} %cot.1, s32[1]{0:T(128)S(6)} %copy.9.counts, s32[1,256]{1,0:T(1,128)} %bitcast.1), custom_call_target="tpu_custom_call" | custom-call | flops 20000000000 | bytes 16777216 | tf_op jit(solution)/shard_map/pallas_call | solution.py:652
  74.3 1.9 %copy.10 = bf16[1,256,1024]{2,1,0:T(8,128)(2,1)} copy(bf16[1,256,1024]{2,1,0:T(8,128)(2,1)} %get-tuple-element.4) | data formatting | bytes 1048576
  76.2 2.3 %copy.11 = f32[1,256,1024]{2,1,0:T(8,128)} copy(f32[1,256,1024]{2,1,0:T(8,128)} %get-tuple-element.5) | data formatting | bytes 2097152

commit v3 on v2

--- a/solution.py
+++ b/solution.py
@@ -350,27 +350,30 @@
                 y_send(p).start()
                 KEEP[p, near_kind(yl)] = KEEP[p, near_kind(yl)] + X2R[p, yl].astype(F32)
 
-        def z_send(p):
-            return rcopy(ZS.at[p - 2], ZR.at[p - 2], z_s.at[p - 2], z_r.at[p - 2], yside)
+        def z_send(p, kind):
+            return rcopy(
+                ZS.at[p - 2, kind], ZR.at[p - 2, kind], z_s.at[p - 2, kind], z_r.at[p - 2, kind], yside
+            )
+
+        far = 1 - keep_kind
 
         def y_late(p):
             core_send(p, 4).wait_recv()
-            for kind in range(2):
+            for kind in (far, keep_kind):
                 ZS[p - 2, kind] = fold(p, 2 * kind + 1 - yl).astype(BF)
-            z_send(p).start()
+                z_send(p, kind).start()
             for kind in range(2):
                 KEEP[p, 2 * kind + yl] = fold(p, 2 * kind + yl)
 
         def x1_late(p):
-            z_send(p).wait_recv()
-            far = 1 - keep_kind
+            z_send(p, far).wait_recv()
             X1S[p, 0] = (KEEP[p, far_kind(yl)] + ZR[p - 2, far].astype(F32)).astype(BF)
             x1_send(p, 1).start()
-            KEEP[p, near_kind(yl)] = KEEP[p, near_kind(yl)] + ZR[p - 2, keep_kind].astype(F32)
 
         def x2_late(p):
+            z_send(p, keep_kind).wait_recv()
             x1_send(p, 1).wait_recv()
-            total = KEEP[p, near_kind(yl)] + X1R[p, 0].astype(F32)
+            total = KEEP[p, near_kind(yl)] + ZR[p - 2, keep_kind].astype(F32) + X1R[p, 0].astype(F32)
             KEEP[p, near_kind(yl)] = total
             X2S[p, 0] = total.astype(BF)
 
@@ -388,27 +391,20 @@
             cols = ds(p, BLK)
             weight_part(p, 2, lambda kind: (KG, VG)[kind][:, cols])
 
-        def early_step(p, carry):
+        def step(p, carry):
             pair(p)
+
+            @pl.when(p == 0)
+            def _():
+                weigh(0)
 
             @pl.when(p == 1)
             def _():
                 x1_early(0)
 
-            weigh(p)
             return carry
 
-        def late_step(p, carry):
-            pair(p)
-
-            @pl.when(p == 2)
-            def _():
-                x1_early(1)
-
-            return carry
-
-        lax.fori_loop(0, 2, early_step, 0)
-        lax.fori_loop(2, 4, late_step, 0)
+        lax.fori_loop(0, 4, step, 0)
 
         def part(d):
             rows = ds(d, BLK)
@@ -417,18 +413,20 @@
                 PS[d, :, out] = (nt(KG[rows], W[0, out]) + nt(VG[rows], W[1, out])).astype(BF)
 
         def first():
+            x2_early(0)
+            weigh(1)
             weigh(2)
-            x2_early(0)
+            x1_early(1)
             weigh(3)
             y_late(2)
 
-        input_parts(part, first, lambda: y_late(3), lambda: x2_early(1))
+        input_parts(part, first, lambda: y_late(3), lambda: y_early(0))
         input_forward()
-        y_early(0)
         x1_late(2)
-        y_early(1)
+        x2_early(1)
         x1_late(3)
         x2_late(2)
+        y_early(1)
         x2_late(3)
         ig[0] = input_total().astype(BF)
 
@@ -451,7 +449,8 @@
             core_send(p, 4).wait_send()
             x1_send(p, n).wait_send()
             if p >= 2:
-                z_send(p).wait_send()
+                z_send(p, 0).wait_send()
+                z_send(p, 1).wait_send()
 
         @pl.when(x >= 2)
         def _():
@@ -551,17 +550,20 @@
         relay_on(0)
         relay(2)
         relay_on(1)
+        spread_end()
+        chunk(0)
         relay(3)
 
         def third():
+            stage_y(0)
+            relay_on(2)
+            chunk(1)
             relay_on(3)
-            spread_end()
-            chunk(0)
-
-        input_parts(part, lambda: relay_on(2), lambda: None, third)
+
+        input_parts(part, lambda: None, lambda: None, third)
         input_forward()
-        stage_y(0)
-        for p in range(1, 4):
+        stage_y(1)
+        for p in range(2, 4):
             chunk(p)
             stage_y(p)
         load_cot.wait()
@@ -644,17 +646,14 @@
         dma((4,)), dma((4,)),
         dma((4,)), dma((4,)),
         dma((4,)), dma((4,)),
-        dma((2,)), dma((2,)),
+        dma((2, 2)), dma((2, 2)),
         dma((6,)), dma((6,)),
     ]
     anywhere = pl.BlockSpec(memory_space=pl.ANY)
     in_vmem = pl.BlockSpec(memory_space=vmem)
     return pl.pallas_call(
         kernel,
-        out_shape=(
-            jax.ShapeDtypeStruct((1, BLK, WIDE), BF),
-            jax.ShapeDtypeStruct((1, BLK, WIDE), F32),
-        ),
+        out_shape=(vmem((1, BLK, WIDE), BF), vmem((1, BLK, WIDE), F32)),
         in_specs=[
             anywhere, anywhere, anywhere,
             pl.BlockSpec(memory_space=pltpu.SMEM),
@@ -663,7 +662,7 @@
         out_specs=(in_vmem, in_vmem),
         scratch_shapes=scratch,
         compiler_params=pltpu.CompilerParams(
-            collective_id=0, has_side_effects=True, vmem_limit_bytes=60 * 2**20
+            collective_id=0, has_side_effects=True, vmem_limit_bytes=56 * 2**20
         ),
         cost_estimate=pl.CostEstimate(
             flops=20 * 10**9, bytes_accessed=16 * 2**20, transcendentals=2**21

time: 78.7 us -> 74.2 us (0.943)
  local copies, waits for them, and re-layouts: 4.17 us -> 1.77 us
  Pallas kernels: 73 us -> 71.1 us
    unnamed x2, local copies, waits for them, and re-layouts: 4.17 us -> 1.77 us
    pallas_call x1, Pallas kernels: 73 us -> 71.1 us  [local(): pl.pallas_call(kernel, out_shape=(vmem((1, BLK, WIDE), BF), vmem((1, BLK,...]
where the time goes in v3:
time: 74.2 us; the launch traced here: 74.1 us
  Pallas kernels  71.1 us (96%)
  local copies, waits for them, and re-layouts  1.77 us (2%)
  between operations  1.29 us (2%)
    pallas_call x1, Pallas kernels, local(): pl.pallas_call(kernel, out_shape=(vmem((1, BLK, WIDE), BF), vmem((1, BLK,...  71.1 us
    unnamed x2, local copies, waits for them, and re-layouts  1.77 us

profile of v3, /device:TPU:17, one launch (start us, length us, event | category | flops | bytes accessed | tf_op | source)
XLA Modules:
  0.0 74.1 jit_solution(15336379281201654383)
XLA Ops:
  1.3 71.1 %shard_map.68 = (bf16[1,256,1024]{2,1,0:T(8,128)(2,1)S(1)}, f32[1,256,1024]{2,1,0:T(8,128)S(1)}) custom-call(bf16[1,256,1024]{2,1,0:T(8,128)(2,1)} %tok.1, bf16[1,4096,1024]{2,1,0:T(8,128)(2,1)} %proj.1, bf16[256,1024]{1,0:T(8,128)(2,1)} %cot.1, s32[1]{0:T(128)S(6)} %copy.11.counts, s32[1,256]{1,0:T(1,128)} %bitcast.1), custom_call_target="tpu_custom_call" | custom-call | flops 20000000000 | bytes 16777216 | tf_op jit(solution)/shard_map/pallas_call | solution.py:654
  72.3 0.8 %copy.9 = bf16[1,256,1024]{2,1,0:T(8,128)(2,1)} copy(bf16[1,256,1024]{2,1,0:T(8,128)(2,1)S(1)} %get-tuple-element.2) | data formatting | bytes 1048576
  73.1 1.0 %copy.10 = f32[1,256,1024]{2,1,0:T(8,128)} copy(f32[1,256,1024]{2,1,0:T(8,128)S(1)} %get-tuple-element.3) | data formatting | bytes 2097152

commit v4 on v3

--- a/solution.py
+++ b/solution.py
@@ -44,8 +44,8 @@
 
 
 def kernel(
-    tok, proj, cot, counts, frames, ig, wg,
-    TOK, W, COT, ACC, Q, U, BIAS, K, KT, V, S, DP, KG, VG, QG, FT, TOKX, QGX,
+    tok, proj, cot, counts_hbm, frames_hbm, ig, wg,
+    counts, frames, TOK, W, COT, ACC, Q, U, BIAS, K, KT, V, S, DP, GR, QG, FT, TOKX, QGX,
     CS, CR, KEEP, X1S, X1R, X2S, X2R, YS, YR, ZS, ZR, PS, RAL, RAR, RBL, RBR,
     l_sem, ag_s, ag_r, q_s, q_r, qg_s, qg_r, aa_s, aa_r, ar_s, ar_r, xg_s, xg_r,
     cs_s, cs_r, x1_s, x1_r, x2_s, x2_r, y_s, y_r, z_s, z_r, rs_s, rs_r,
@@ -91,6 +91,10 @@
             load_w(i, i).start()
 
     load_cot.start()
+    load_counts = pltpu.make_async_copy(counts_hbm, counts, l_sem.at[6])
+    load_frames = pltpu.make_async_copy(frames_hbm, frames, l_sem.at[7])
+    load_counts.start()
+    load_frames.start()
 
     barrier = pltpu.get_barrier_semaphore()
     greet = [right, left, partner, core, yside] + [xdev((x + d) % 4) for d in (1, 2, 3)]
@@ -189,6 +193,9 @@
     ring(1, 3, right_m).wait_recv()
     project(right_m, 2, 1)
 
+    load_counts.wait()
+    load_frames.wait()
+
     @pl.when(is_video)
     def _():
         load_cot.wait()
@@ -203,28 +210,25 @@
     ring(1, 5, far_m).wait_recv()
     project(far_m, 3, 1)
 
-    def core_send(p, count):
-        return rcopy(CS.at[p, pl.ds(0, count)], CR.at[p, pl.ds(0, count)], cs_s.at[p], cs_r.at[p], core)
-
-    def weight_part(p, kinds, rhs):
-        for kind in range(kinds):
-            for yd in range(2):
-                CS[p, kind * 2 + yd] = nn(FT[ds(2 * yd + 1 - c, BLK)], rhs(kind)).astype(BF)
-        core_send(p, 2 * kinds).start()
-        for kind in range(kinds):
-            for yd in range(2):
-                KEEP[p, kind * 2 + yd] = nn(FT[ds(2 * yd + c, BLK)], rhs(kind))
+    def core_send(p, kind):
+        both = pl.ds(2 * kind, 2)
+        return rcopy(CS.at[p, both], CR.at[p, both], cs_s.at[p, kind], cs_r.at[p, kind], core)
+
+    def weight_part(p, kind, rhs):
+        for yd in range(2):
+            CS[p, kind * 2 + yd] = nn(FT[ds(2 * yd + 1 - c, BLK)], rhs).astype(BF)
+        core_send(p, kind).start()
+        for yd in range(2):
+            KEEP[p, kind * 2 + yd] = nn(FT[ds(2 * yd + c, BLK)], rhs)
 
     def y_send(p):
         return rcopy(YS.at[p], YR.at[p], y_s.at[p], y_r.at[p], yside)
 
-    def x1_send(p, n):
-        some = pl.ds(0, n)
-        return rcopy(X1S.at[p, some], X1R.at[p, some], x1_s.at[p], x1_r.at[p], xnear)
-
-    def x2_send(p, n):
-        some = pl.ds(0, n)
-        return rcopy(X2S.at[p, some], X2R.at[p, some], x2_s.at[p], x2_r.at[p], xback)
+    def x1_send(p, i):
+        return rcopy(X1S.at[p, i], X1R.at[p, i], x1_s.at[p, i], x1_r.at[p, i], xnear)
+
+    def x2_send(p, i):
+        return rcopy(X2S.at[p, i], X2R.at[p, i], x2_s.at[p, i], x2_r.at[p, i], xback)
 
     def part_send(i):
         src = (
@@ -260,8 +264,11 @@
             part_send(i).wait_recv()
         return PS[m].astype(F32) + RBL[...].astype(F32) + RBR[...].astype(F32)
 
-    def qg_send(p):
-        return rcopy(QG.at[p], QGX.at[p, ds(x, BLK)], qg_s.at[p], qg_r.at[p], partner)
+    def qg_send(p, hh):
+        return rcopy(
+            QG.at[p, hh], QGX.at[p, ds(x, BLK), pl.ds(hh * HALF, HALF)],
+            qg_s.at[p, hh], qg_r.at[p, hh], partner,
+        )
 
     @pl.when(is_video)
     def _():
@@ -300,12 +307,13 @@
                 query_grad = None
                 for t in range(4):
                     a = S[4 * hh + t] * inverse
-                    VG[blocks[t], cols] = nn(a.astype(BF), u).astype(BF)
+                    GR[1, blocks[t], cols] = nn(a.astype(BF), u).astype(BF)
                     sg = (a * (DP[4 * hh + t] - mean) * FACTOR).astype(BF)
-                    KG[blocks[t], cols] = nn(sg, q).astype(BF)
+                    GR[0, blocks[t], cols] = nn(sg, q).astype(BF)
                     more = nn(KT[cols, blocks[t]], sg)
                     query_grad = more if query_grad is None else query_grad + more
-                QG[p, :, head] = query_grad.T.astype(BF)
+                QG[p, hh] = query_grad.T.astype(BF)
+                qg_send(p, hh).start()
 
             cols0, head0, q0, u0, top0 = scores(0)
             inverse0, mean0 = weights(0, cols0, u0, top0)
@@ -314,6 +322,8 @@
             inverse1, mean1 = weights(1, cols1, u1, top1)
             grads(1, cols1, head1, q1, u1, inverse1, mean1)
 
+        far = 1 - keep_kind
+
         def fold(p, i):
             return KEEP[p, i] + CR[p, i].astype(F32)
 
@@ -324,72 +334,66 @@
             return keep_kind * 2 + yd
 
         def x1_early(p):
-            core_send(p, 4).wait_recv()
-            for yd in range(2):
-                X1S[p, yd] = fold(p, far_kind(yd)).astype(BF)
-            x1_send(p, 2).start()
-            for yd in range(2):
-                KEEP[p, near_kind(yd)] = fold(p, near_kind(yd))
-
-        def x2_early(p):
-            x1_send(p, 2).wait_recv()
-            for yd in range(2):
-                total = KEEP[p, near_kind(yd)] + X1R[p, yd].astype(F32)
-                KEEP[p, near_kind(yd)] = total
-                X2S[p, yd] = total.astype(BF)
+            core_send(p, far).wait_recv()
+            for i, yd in ((0, 1 - yl), (1, yl)):
+                X1S[p, i] = fold(p, far_kind(yd)).astype(BF)
+                x1_send(p, i).start()
+
+        def x2_early(p, i):
+            if i == 0:
+                core_send(p, keep_kind).wait_recv()
+            yd = (1 - yl, yl)[i]
+            x1_send(p, i).wait_recv()
+            total = fold(p, near_kind(yd)) + X1R[p, i].astype(F32)
+            KEEP[p, near_kind(yd)] = total
+            X2S[p, i] = total.astype(BF)
 
             @pl.when(x >= 2)
             def _():
-                x2_send(p, 2).start()
+                x2_send(p, i).start()
 
         def y_early(p):
             @pl.when(x < 2)
             def _():
-                x2_send(p, 2).wait_recv()
-                YS[p] = (KEEP[p, near_kind(1 - yl)] + X2R[p, 1 - yl].astype(F32)).astype(BF)
+                x2_send(p, 0).wait_recv()
+                YS[p] = (KEEP[p, near_kind(1 - yl)] + X2R[p, 0].astype(F32)).astype(BF)
                 y_send(p).start()
-                KEEP[p, near_kind(yl)] = KEEP[p, near_kind(yl)] + X2R[p, yl].astype(F32)
 
         def z_send(p, kind):
             return rcopy(
                 ZS.at[p - 2, kind], ZR.at[p - 2, kind], z_s.at[p - 2, kind], z_r.at[p - 2, kind], yside
             )
 
-        far = 1 - keep_kind
-
-        def y_late(p):
-            core_send(p, 4).wait_recv()
-            for kind in (far, keep_kind):
-                ZS[p - 2, kind] = fold(p, 2 * kind + 1 - yl).astype(BF)
-                z_send(p, kind).start()
-            for kind in range(2):
-                KEEP[p, 2 * kind + yl] = fold(p, 2 * kind + yl)
+        def y_late(p, kind):
+            core_send(p, kind).wait_recv()
+            ZS[p - 2, kind] = fold(p, 2 * kind + 1 - yl).astype(BF)
+            z_send(p, kind).start()
+            KEEP[p, 2 * kind + yl] = fold(p, 2 * kind + yl)
 
         def x1_late(p):
             z_send(p, far).wait_recv()
             X1S[p, 0] = (KEEP[p, far_kind(yl)] + ZR[p - 2, far].astype(F32)).astype(BF)
-            x1_send(p, 1).start()
+            x1_send(p, 0).start()
 
         def x2_late(p):
             z_send(p, keep_kind).wait_recv()
-            x1_send(p, 1).wait_recv()
+            x1_send(p, 0).wait_recv()
             total = KEEP[p, near_kind(yl)] + ZR[p - 2, keep_kind].astype(F32) + X1R[p, 0].astype(F32)
             KEEP[p, near_kind(yl)] = total
             X2S[p, 0] = total.astype(BF)
 
             @pl.when(x >= 2)
             def _():
-                x2_send(p, 1).start()
+                x2_send(p, 0).start()
 
         def pair(p):
             for half in range(2):
                 q_send(p, half).wait_recv()
             attend(p)
-            qg_send(p).start()
 
         def weigh(p):
-            cols = ds(p, BLK)
-            weight_part(p, 2, lambda kind: (KG, VG)[kind][:, cols])
+            for kind in (far, keep_kind):
+                weight_part(p, kind, GR[kind, :, ds(p, BLK)])
 
         def step(p, carry):
             pair(p)
@@ -410,33 +414,43 @@
             rows = ds(d, BLK)
             for j in range(4):
                 out = pl.ds(j * BLK, BLK)
-                PS[d, :, out] = (nt(KG[rows], W[0, out]) + nt(VG[rows], W[1, out])).astype(BF)
+                PS[d, :, out] = (nt(GR[0, rows], W[0, out]) + nt(GR[1, rows], W[1, out])).astype(BF)
 
         def first():
-            x2_early(0)
+            x2_early(0, 0)
             weigh(1)
+            x1_early(1)
+            x2_early(0, 1)
             weigh(2)
-            x1_early(1)
+            y_late(2, far)
             weigh(3)
-            y_late(2)
-
-        input_parts(part, first, lambda: y_late(3), lambda: y_early(0))
+            y_late(3, far)
+            y_late(2, keep_kind)
+
+        def second():
+            x2_early(1, 0)
+            y_late(3, keep_kind)
+
+        input_parts(part, first, second, lambda: y_early(0))
         input_forward()
         x1_late(2)
-        x2_early(1)
+        x2_early(1, 1)
         x1_late(3)
+        y_early(1)
         x2_late(2)
-        y_early(1)
         x2_late(3)
         ig[0] = input_total().astype(BF)
 
         @pl.when(x < 2)
         def _():
             for p in range(2):
+                x2_send(p, 1).wait_recv()
                 y_send(p).wait_recv()
-                wg[0, :, pl.ds(p * BLK, BLK)] = KEEP[p, near_kind(yl)] + YR[p].astype(F32)
+                wg[0, :, pl.ds(p * BLK, BLK)] = (
+                    KEEP[p, near_kind(yl)] + X2R[p, 1].astype(F32) + YR[p].astype(F32)
+                )
             for p in range(2, 4):
-                x2_send(p, 1).wait_recv()
+                x2_send(p, 0).wait_recv()
                 wg[0, :, pl.ds(p * BLK, BLK)] = KEEP[p, near_kind(yl)] + X2R[p, 0].astype(F32)
 
         @pl.when(x >= 2)
@@ -445,9 +459,11 @@
 
         for p in range(4):
             n = 2 if p < 2 else 1
-            qg_send(p).wait_send()
-            core_send(p, 4).wait_send()
-            x1_send(p, n).wait_send()
+            for i in range(2):
+                qg_send(p, i).wait_send()
+                core_send(p, i).wait_send()
+            for i in range(n):
+                x1_send(p, i).wait_send()
             if p >= 2:
                 z_send(p, 0).wait_send()
                 z_send(p, 1).wait_send()
@@ -455,7 +471,8 @@
         @pl.when(x >= 2)
         def _():
             for p in range(4):
-                x2_send(p, 2 if p < 2 else 1).wait_send()
+                for i in range(2 if p < 2 else 1):
+                    x2_send(p, i).wait_send()
 
         @pl.when(x < 2)
         def _():
@@ -503,28 +520,32 @@
         right_x, left_x, far_x = (x + 1) % 4, (x + 3) % 4, (x + 2) % 4
 
         def gather(p, i, block):
-            rows = (ds(block, BLK), ds(block, BLK), ds(2 * block, HALF), ds(2 * block + 1, HALF))[i]
-            s = QGX.at[p, rows]
+            rows = ds(block, BLK) if i < 4 else ds(2 * block + i - 4, HALF)
+            cols = pl.ds((i // 2) * HALF, HALF) if i < 4 else pl.ds(0, BLK)
+            s = QGX.at[p, rows, cols]
             return rcopy(s, s, xg_s.at[p, i], xg_r.at[p, i], xdev(right_x if i % 2 == 0 else left_x))
 
         def relay(p):
-            qg_send(p).wait_recv()
-            gather(p, 0, x).start()
-            gather(p, 1, x).start()
+            for hh in range(2):
+                qg_send(p, hh).wait_recv()
+                gather(p, 2 * hh, x).start()
+                gather(p, 2 * hh + 1, x).start()
 
         def relay_on(p):
             gather(p, 0, left_x).wait_recv()
-            gather(p, 2, left_x).start()
+            gather(p, 2, left_x).wait_recv()
+            gather(p, 4, left_x).start()
             gather(p, 1, right_x).wait_recv()
-            gather(p, 3, right_x).start()
+            gather(p, 3, right_x).wait_recv()
+            gather(p, 5, right_x).start()
 
         def chunk(p):
-            gather(p, 2, far_x).wait_recv()
-            gather(p, 3, far_x).wait_recv()
-            weight_part(p, 1, lambda kind: QGX[p])
+            gather(p, 4, far_x).wait_recv()
+            gather(p, 5, far_x).wait_recv()
+            weight_part(p, 0, QGX[p])
 
         def stage_y(p):
-            core_send(p, 2).wait_recv()
+            core_send(p, 0).wait_recv()
             YS[p] = (KEEP[p, 1 - yl] + CR[p, 1 - yl].astype(F32)).astype(BF)
             y_send(p).start()
             KEEP[p, yl] = KEEP[p, yl] + CR[p, yl].astype(F32)
@@ -545,39 +566,39 @@
         spread_start(1)
         spread_on(0)
         relay(0)
+        relay(1)
         spread_on(1)
-        relay(1)
         relay_on(0)
         relay(2)
-        relay_on(1)
-        spread_end()
-        chunk(0)
         relay(3)
 
         def third():
+            spread_end()
+            chunk(0)
+            relay_on(2)
             stage_y(0)
-            relay_on(2)
-            chunk(1)
-            relay_on(3)
-
-        input_parts(part, lambda: None, lambda: None, third)
+
+        input_parts(part, lambda: relay_on(1), lambda: None, third)
         input_forward()
+        chunk(1)
+        relay_on(3)
         stage_y(1)
-        for p in range(2, 4):
-            chunk(p)
-            stage_y(p)
+        chunk(2)
+        chunk(3)
+        stage_y(2)
+        stage_y(3)
         load_cot.wait()
         ig[0] = (input_total() + COT[...].astype(F32)).astype(BF)
         for p in range(4):
             y_send(p).wait_recv()
             wg[0, :, pl.ds(p * BLK, BLK)] = KEEP[p, yl] + YR[p].astype(F32)
         for p in range(4):
-            core_send(p, 2).wait_send()
+            core_send(p, 0).wait_send()
             y_send(p).wait_send()
-            gather(p, 0, x).wait_send()
-            gather(p, 1, x).wait_send()
-            gather(p, 2, left_x).wait_send()
-            gather(p, 3, right_x).wait_send()
+            for i in range(4):
+                gather(p, i, x).wait_send()
+            gather(p, 4, left_x).wait_send()
+            gather(p, 5, right_x).wait_send()
             for half in range(2):
                 q_send(p, half).wait_send()
         for half in range(2):
@@ -601,6 +622,8 @@
     vmem = pltpu.VMEM
     dma = pltpu.SemaphoreType.DMA
     scratch = [
+        pltpu.SMEM((1,), jnp.int32),
+        vmem((1, BLK), jnp.int32),
         vmem((4, BLK, WIDE), BF),
         vmem((4, WIDE, WIDE), BF),
         vmem((BLK, WIDE), BF),
@@ -613,9 +636,8 @@
         vmem((WIDE, WIDE), BF),
         vmem((8, BLK, BLK), F32),
         vmem((8, BLK, BLK), F32),
-        vmem((WIDE, WIDE), BF),
-        vmem((WIDE, WIDE), BF),
-        vmem((4, BLK, BLK), BF),
+        vmem((2, WIDE, WIDE), BF),
+        vmem((4, 2, BLK, HALF), BF),
         vmem((WIDE, WIDE), BF),
         vmem((4, BLK, WIDE), BF),
         vmem((4, WIDE, BLK), BF),
@@ -635,16 +657,16 @@
         vmem((HALF, WIDE), BF),
         vmem((BLK, WIDE), BF),
         vmem((BLK, WIDE), BF),
-        dma((6,)),
+        dma((8,)),
         dma((2, 6)), dma((2, 6)),
         dma((4, 2)), dma((4, 2)),
-        dma((4,)), dma((4,)),
+        dma((4, 2)), dma((4, 2)),
         dma((2, 3)), dma((2, 3)),
         dma((2, 3, 4)), dma((2, 3, 4)),
-        dma((4, 4)), dma((4, 4)),
-        dma((4,)), dma((4,)),
-        dma((4,)), dma((4,)),
-        dma((4,)), dma((4,)),
+        dma((4, 6)), dma((4, 6)),
+        dma((4, 2)), dma((4, 2)),
+        dma((4, 2)), dma((4, 2)),
+        dma((4, 2)), dma((4, 2)),
         dma((4,)), dma((4,)),
         dma((2, 2)), dma((2, 2)),
         dma((6,)), dma((6,)),
@@ -655,9 +677,7 @@
         kernel,
         out_shape=(vmem((1, BLK, WIDE), BF), vmem((1, BLK, WIDE), F32)),
         in_specs=[
-            anywhere, anywhere, anywhere,
-            pl.BlockSpec(memory_space=pltpu.SMEM),
-            in_vmem,
+            anywhere, anywhere, anywhere, anywhere, anywhere,
         ],
         out_specs=(in_vmem, in_vmem),
         scratch_shapes=scratch,

time: 74.2 us -> 72.9 us (0.982); the launches traced: 74.1 us -> 72 us
  Pallas kernels: 71.1 us -> 68.9 us
    pallas_call x1, Pallas kernels: 71.1 us -> 68.9 us  [local(): pl.pallas_call(kernel, out_shape=(vmem((1, BLK, WIDE), BF), vmem((1, BLK,...]
where the time goes in v4:
time: 72.9 us; the launch traced here: 72 us
  Pallas kernels  68.9 us (95%)
  local copies, waits for them, and re-layouts  1.77 us (2%)
  between operations  1.29 us (2%)
    pallas_call x1, Pallas kernels, local(): pl.pallas_call(kernel, out_shape=(vmem((1, BLK, WIDE), BF), vmem((1, BLK,...  68.9 us
    unnamed x2, local copies, waits for them, and re-layouts  1.77 us

profile of v4, /device:TPU:17, one launch (start us, length us, event | category | flops | bytes accessed | tf_op | source)
XLA Modules:
  0.0 72.0 jit_solution(853384665128562692)
XLA Ops:
  1.3 68.9 %shard_map.68 = (bf16[1,256,1024]{2,1,0:T(8,128)(2,1)S(1)}, f32[1,256,1024]{2,1,0:T(8,128)S(1)}) custom-call(bf16[1,256,1024]{2,1,0:T(8,128)(2,1)} %tok.1, bf16[1,4096,1024]{2,1,0:T(8,128)(2,1)} %proj.1, bf16[256,1024]{1,0:T(8,128)(2,1)} %cot.1, s32[1]{0:T(128)S(6)} %copy.11.counts_hbm, s32[1,256]{1,0:T(1,128)} %bitcast.1), custom_call_target="tpu_custom_call" | custom-call | flops 20000000000 | bytes 16777216 | tf_op jit(solution)/shard_map/pallas_call | solution.py:676
  70.2 0.8 %copy.9 = bf16[1,256,1024]{2,1,0:T(8,128)(2,1)} copy(bf16[1,256,1024]{2,1,0:T(8,128)(2,1)S(1)} %get-tuple-element.2) | data formatting | bytes 1048576
  71.0 1.0 %copy.10 = f32[1,256,1024]{2,1,0:T(8,128)} copy(f32[1,256,1024]{2,1,0:T(8,128)S(1)} %get-tuple-element.3) | data formatting | bytes 2097152

commit v5 on v4

--- a/solution.py
+++ b/solution.py
@@ -45,7 +45,7 @@
 
 def kernel(
     tok, proj, cot, counts_hbm, frames_hbm, ig, wg,
-    counts, frames, TOK, W, COT, ACC, Q, U, BIAS, K, KT, V, S, DP, GR, QG, FT, TOKX, QGX,
+    counts, frames, TOK, W, COT, ACC, Q, U, BIAS, K, KT, V, S, DP, GR, QG, FT, TOKX, QGX, PSUM,
     CS, CR, KEEP, X1S, X1R, X2S, X2R, YS, YR, ZS, ZR, PS, RAL, RAR, RBL, RBR,
     l_sem, ag_s, ag_r, q_s, q_r, qg_s, qg_r, aa_s, aa_r, ar_s, ar_r, xg_s, xg_r,
     cs_s, cs_r, x1_s, x1_r, x2_s, x2_r, y_s, y_r, z_s, z_r, rs_s, rs_r,
@@ -418,11 +418,11 @@
 
         def first():
             x2_early(0, 0)
+            weigh(2)
+            y_late(2, far)
             weigh(1)
             x1_early(1)
             x2_early(0, 1)
-            weigh(2)
-            y_late(2, far)
             weigh(3)
             y_late(3, far)
             y_late(2, keep_kind)
@@ -550,14 +550,27 @@
             y_send(p).start()
             KEEP[p, yl] = KEEP[p, yl] + CR[p, yl].astype(F32)
 
+        def some_part(d, j, pairs):
+            total = None
+            for p in pairs:
+                more = nt(QGX[p, ds(x, BLK)], W[d, pl.ds(j * BLK, BLK), pl.ds(p * BLK, BLK)])
+                total = more if total is None else total + more
+            return total
+
+        def begin_parts(d, carry):
+            for j in range(4):
+                PSUM[d, :, pl.ds(j * BLK, BLK)] = some_part(d, j, (0, 1))
+            return carry
+
+        def add_parts(d, carry):
+            for j in range(4):
+                PSUM[d, :, pl.ds(j * BLK, BLK)] += some_part(d, j, (2,))
+            return carry
+
         def part(d):
             for j in range(4):
                 out = pl.ds(j * BLK, BLK)
-                total = None
-                for p in range(4):
-                    more = nt(QGX[p, ds(x, BLK)], W[d, out, pl.ds(p * BLK, BLK)])
-                    total = more if total is None else total + more
-                PS[d, :, out] = total.astype(BF)
+                PS[d, :, out] = (PSUM[d, :, out] + some_part(d, j, (3,))).astype(BF)
 
         for d in (1, 3, 2):
             swap_send(1, d).start()
@@ -567,9 +580,11 @@
         spread_on(0)
         relay(0)
         relay(1)
+        lax.fori_loop(0, 4, begin_parts, 0)
         spread_on(1)
         relay_on(0)
         relay(2)
+        lax.fori_loop(0, 4, add_parts, 0)
         relay(3)
 
         def third():
@@ -641,6 +656,7 @@
         vmem((WIDE, WIDE), BF),
         vmem((4, BLK, WIDE), BF),
         vmem((4, WIDE, BLK), BF),
+        vmem((4, BLK, WIDE), F32),
         vmem((4, 4, BLK, BLK), BF),
         vmem((4, 4, BLK, BLK), BF),
         vmem((4, 4, BLK, BLK), F32),

time: 72.9 us -> 72.5 us (level)
  no operation moved by 1% of the time
where the time goes in v5:
time: 72.5 us; the launch traced here: 71.6 us
  Pallas kernels  68.5 us (94%)
  local copies, waits for them, and re-layouts  1.77 us (2%)
  between operations  1.29 us (2%)
    pallas_call x1, Pallas kernels, local(): pl.pallas_call(kernel, out_shape=(vmem((1, BLK, WIDE), BF), vmem((1, BLK,...  68.5 us
    unnamed x2, local copies, waits for them, and re-layouts  1.77 us

profile of v5, /device:TPU:17, one launch (start us, length us, event | category | flops | bytes accessed | tf_op | source)
XLA Modules:
  0.0 71.6 jit_solution(4716000318306398309)
XLA Ops:
  1.3 68.5 %shard_map.68 = (bf16[1,256,1024]{2,1,0:T(8,128)(2,1)S(1)}, f32[1,256,1024]{2,1,0:T(8,128)S(1)}) custom-call(bf16[1,256,1024]{2,1,0:T(8,128)(2,1)} %tok.1, bf16[1,4096,1024]{2,1,0:T(8,128)(2,1)} %proj.1, bf16[256,1024]{1,0:T(8,128)(2,1)} %cot.1, s32[1]{0:T(128)S(6)} %copy.11.counts_hbm, s32[1,256]{1,0:T(1,128)} %bitcast.1), custom_call_target="tpu_custom_call" | custom-call | flops 20000000000 | bytes 16777216 | tf_op jit(solution)/shard_map/pallas_call | solution.py:692
  69.8 0.8 %copy.9 = bf16[1,256,1024]{2,1,0:T(8,128)(2,1)} copy(bf16[1,256,1024]{2,1,0:T(8,128)(2,1)S(1)} %get-tuple-element.2) | data formatting | bytes 1048576
  70.6 1.0 %copy.10 = f32[1,256,1024]{2,1,0:T(8,128)} copy(f32[1,256,1024]{2,1,0:T(8,128)S(1)} %get-tuple-element.3) | data formatting | bytes 2097152

commit v6 on v5

--- a/solution.py
+++ b/solution.py
@@ -428,8 +428,8 @@
             y_late(2, keep_kind)
 
         def second():
+            y_late(3, keep_kind)
             x2_early(1, 0)
-            y_late(3, keep_kind)
 
         input_parts(part, first, second, lambda: y_early(0))
         input_forward()

time: 72.5 us -> 72.5 us (level)
  no operation moved by 1% of the time
where the time goes in v6:
time: 72.5 us; the launch traced here: 71.6 us
  Pallas kernels  68.5 us (94%)
  local copies, waits for them, and re-layouts  1.77 us (2%)
  between operations  1.29 us (2%)
    pallas_call x1, Pallas kernels, local(): pl.pallas_call(kernel, out_shape=(vmem((1, BLK, WIDE), BF), vmem((1, BLK,...  68.5 us
    unnamed x2, local copies, waits for them, and re-layouts  1.77 us

profile of v6, /device:TPU:17, one launch (start us, length us, event | category | flops | bytes accessed | tf_op | source)
XLA Modules:
  0.0 71.6 jit_solution(5475693678697242993)
XLA Ops:
  1.3 68.5 %shard_map.68 = (bf16[1,256,1024]{2,1,0:T(8,128)(2,1)S(1)}, f32[1,256,1024]{2,1,0:T(8,128)S(1)}) custom-call(bf16[1,256,1024]{2,1,0:T(8,128)(2,1)} %tok.1, bf16[1,4096,1024]{2,1,0:T(8,128)(2,1)} %proj.1, bf16[256,1024]{1,0:T(8,128)(2,1)} %cot.1, s32[1]{0:T(128)S(6)} %copy.11.counts_hbm, s32[1,256]{1,0:T(1,128)} %bitcast.1), custom_call_target="tpu_custom_call" | custom-call | flops 20000000000 | bytes 16777216 | tf_op jit(solution)/shard_map/pallas_call | solution.py:692
  69.8 0.8 %copy.9 = bf16[1,256,1024]{2,1,0:T(8,128)(2,1)} copy(bf16[1,256,1024]{2,1,0:T(8,128)(2,1)S(1)} %get-tuple-element.2) | data formatting | bytes 1048576
  70.6 1.0 %copy.10 = f32[1,256,1024]{2,1,0:T(8,128)} copy(f32[1,256,1024]{2,1,0:T(8,128)S(1)} %get-tuple-element.3) | data formatting | bytes 2097152
